TPU v7x, 128 devices: a whole 4x4x4 slice. The times are simulated.
128 devices in a mesh: gx: 16 (over z, y), gy: 8 (over x, core).
Axes of the slice: x: 4, y: 4, z: 4, core: 2. Of those that a mesh axis runs over, the one named last changes fastest.
Arguments:
- positions: float32 [3, 32768, 128], P(None, ('gx', 'gy')), may hold values from 0 to 1
- masses: float32 [32768, 128], P(('gx', 'gy')), may hold values from 0.004 to 0.012
- smoothing: float32 [32768, 128], P(('gx', 'gy')), may hold values from 0.55 to 1
- entropy: float32 [32768, 128], P(('gx', 'gy')), may hold values from 0.5 to 2
- density: float32 [32768, 128], P(('gx', 'gy')), may hold values from 0.5 to 2
- active_cells: int32 [512], P(('gx', 'gy')), may hold values from 0 to 32767, as said below
- active_count: int32 [128], P(('gx', 'gy')), may hold values from 1 to 4, 324 in all
- neighbours: int32 [512, 27], P(('gx', 'gy')), may hold values from 0 to 32767, as said below
- mig_source: int32 [16384], P(('gx', 'gy')), may hold values from 0 to 32767
- mig_dest: int32 [16384, 1], P(('gx', 'gy')), may hold values from 0 to 127; in each aligned block of 128 rows (0 to 127, 128 to 255, ...) at most 2 rows name the same one
Outputs:
- new_density: float32 [32768, 128], P(('gx', 'gy'))
- acceleration: float32 [3, 512, 128], P(None, ('gx', 'gy'))
- arrivals: float32 [7, 32768], P(None, ('gx', 'gy'))
Inputs may be any that keep to these rules, and one draw needn't show every extreme that they name: `active_cells`: the 4 entries of device d are distinct cells of device d. The middle entry (index 13) of a slot is its active cell. Every other entry is a cell of the slot's own device, or a cell of the device just before or just after it in the cell order lying within 64 cells of the end they share. Over all slots of one device, at most 8 distinct cells of each of these two devices are named, and every device with neighbours on both sides names exactly 8 on each side. `mig_dest`: within the 128 rows of one device no destination appears more than 2 times; some destination appears exactly 2 times.
All inputs are finite; a program needn't handle non-finite values. No bound on the sum of `active_count` on one device may be relied on, other than what follows from the above.
Results may differ from a plain program's by a relative error of at most 0.0003.
Values sent between devices are 32-bit elements; how exact they have to be, the bound alone decides.
A program may use at most 64 MiB of HBM per device.

v0:
```python
import math

import jax
import jax.numpy as jnp
from jax import lax
from jax.sharding import PartitionSpec as P

P_SIZE = 128
NBR = 27
RIM = 64


kernel_norm = 8.0 / math.pi


def padded(block, sides, width):
    for axis, dim in sides:
        count = lax.axis_size(axis)
        forward = [(i, i + 1) for i in range(count - 1)]
        backward = [(target, source) for source, target in forward]
        low = lax.ppermute(
            lax.slice_in_dim(block, block.shape[dim] - width, None, axis=dim), axis, forward
        )
        high = lax.ppermute(lax.slice_in_dim(block, 0, width, axis=dim), axis, backward)
        block = jnp.concatenate([low, block, high], axis=dim)
    return block


def stencil_offsets():
    index = jnp.arange(NBR)
    return jnp.stack([index // 9 - 1, index // 3 % 3 - 1, index % 3 - 1]).astype(jnp.float32)


def kernel_value(ratio):
    inner = 1.0 - 6.0 * ratio * ratio + 6.0 * ratio * ratio * ratio
    outer = 2.0 * (1.0 - ratio) ** 3
    return jnp.where(ratio < 0.5, inner, jnp.where(ratio < 1.0, outer, 0.0))


def kernel_slope(ratio):
    safe_ratio = jnp.maximum(ratio, 0.5)
    inner = -12.0 + 18.0 * ratio
    outer = -6.0 * (1.0 - ratio) ** 2 / safe_ratio
    return jnp.where(ratio < 0.5, inner, jnp.where(ratio < 1.0, outer, 0.0))


def pair_geometry(own_pos, other_pos):
    separation = own_pos[:, :, None, None] - other_pos[:, None, :, :]
    distance = jnp.sqrt(jnp.sum(separation * separation, axis=0))
    return (separation, distance)


def density_cell(own_pos, own_len, other_pos, other_mass):
    separation, distance = pair_geometry(own_pos, other_pos)
    weights = kernel_value(distance / own_len[:, None, None])
    return kernel_norm * jnp.sum(other_mass[None] * weights, axis=(1, 2)) / own_len**3


def force_cell(
    own_pos, own_len, own_rho, own_press, other_pos, other_mass, other_len, other_rho, other_press
):
    separation, distance = pair_geometry(own_pos, other_pos)
    own_term = (own_press / own_rho**2 * kernel_norm / own_len**5)[
        :, None, None
    ] * kernel_slope(distance / own_len[:, None, None])
    other_term = (other_press / other_rho**2 * kernel_norm / other_len**5)[None] * kernel_slope(
        distance / other_len[None]
    )
    factor = other_mass[None] * (own_term + other_term)
    return -jnp.sum(factor[None] * separation, axis=(2, 3))


def gather_slots(table_pos, lookup_ids, stencil):
    near_pos = jnp.take(table_pos, lookup_ids, axis=1) + stencil[:, None, :, None]
    return jnp.moveaxis(near_pos, 1, 0)


def local(
    positions,
    masses,
    smoothing,
    entropy,
    density,
    active_cells,
    active_count,
    neighbours,
    mig_source,
    mig_dest,
):
    cell_count = masses.shape[0]
    slot_count = active_cells.shape[0]
    my_index = lax.axis_index(("gx", "gy"))
    devices = lax.axis_size(("gx", "gy"))
    stencil = stencil_offsets()
    local_active = active_cells - my_index * cell_count
    near_index = neighbours - (my_index * cell_count - RIM)
    live_slot = jnp.arange(slot_count) < active_count[0]
    first_rows = jnp.concatenate([positions, masses[None]], axis=0)
    extended = padded(first_rows, ((("gx", "gy"), 1),), RIM)
    own_pos = jnp.moveaxis(jnp.take(positions, local_active, axis=1), 1, 0)
    own_len = smoothing[local_active]
    near_pos = gather_slots(extended[0:3], near_index, stencil)
    near_mass = extended[3][near_index]

    def density_one(inputs):
        cell_pos, cell_len, other_pos, other_mass = inputs
        return density_cell(cell_pos, cell_len, other_pos, other_mass)

    rho = lax.map(density_one, (own_pos, own_len, near_pos, near_mass))
    kept = jnp.where(live_slot[:, None], rho, density[local_active])
    new_density = density.at[local_active].set(kept)
    pressure = entropy * jnp.exp(5.0 / 3.0 * jnp.log(new_density))
    state_rows = jnp.concatenate(
        [positions, masses[None], smoothing[None], new_density[None], pressure[None]], axis=0
    )
    ghost_all = padded(state_rows, ((("gx", "gy"), 1),), RIM)
    force_pos = gather_slots(ghost_all[0:3], near_index, stencil)
    force_mass = ghost_all[3][near_index]
    force_len = ghost_all[4][near_index]
    force_rho = ghost_all[5][near_index]
    force_press = ghost_all[6][near_index]
    own_rho = new_density[local_active]
    own_press = pressure[local_active]

    def force_one(inputs):
        (
            cell_pos,
            cell_len,
            cell_rho,
            cell_press,
            other_pos,
            other_mass,
            other_len,
            other_rho,
            other_press,
        ) = inputs
        return force_cell(
            cell_pos,
            cell_len,
            cell_rho,
            cell_press,
            other_pos,
            other_mass,
            other_len,
            other_rho,
            other_press,
        )

    accel_rows = lax.map(
        force_one,
        (
            own_pos,
            own_len,
            own_rho,
            own_press,
            force_pos,
            force_mass,
            force_len,
            force_rho,
            force_press,
        ),
    )
    acceleration = jnp.transpose(accel_rows, (1, 0, 2)) * live_slot[None, :, None].astype(
        jnp.float32
    )
    mig_rows = mig_source.shape[0]
    capacity = max(2, 2 * mig_rows // devices)
    flat_count = cell_count * P_SIZE
    payload = jnp.concatenate(
        [
            positions.reshape(3, flat_count)[:, mig_source],
            masses.reshape(flat_count)[mig_source][None],
            smoothing.reshape(flat_count)[mig_source][None],
            entropy.reshape(flat_count)[mig_source][None],
            new_density.reshape(flat_count)[mig_source][None],
        ],
        axis=0,
    )
    destination = mig_dest[:, 0]
    same = destination[:, None] == destination[None, :]
    earlier = jnp.arange(mig_rows)[None, :] < jnp.arange(mig_rows)[:, None]
    slot_rank = jnp.sum(jnp.logical_and(same, earlier), axis=1)
    column = destination * capacity + slot_rank
    outgoing = jnp.zeros((7, devices * capacity), jnp.float32).at[:, column].set(payload)
    arrivals = lax.all_to_all(outgoing, ("gx", "gy"), split_axis=1, concat_axis=1, tiled=True)
    return (new_density, acceleration, arrivals)


def solution(mesh):
    placed = (
        P(None, ("gx", "gy"), None),
        P(("gx", "gy"), None),
        P(("gx", "gy"), None),
        P(("gx", "gy"), None),
        P(("gx", "gy"), None),
        P(("gx", "gy")),
        P(("gx", "gy")),
        P(("gx", "gy"), None),
        P(("gx", "gy")),
        P(("gx", "gy"), None),
    )
    return jax.shard_map(
        local,
        mesh=mesh,
        in_specs=placed,
        out_specs=(P(("gx", "gy"), None), P(None, ("gx", "gy"), None), P(None, ("gx", "gy"))),
        check_vma=False,
    )
```

profile of v0, /device:TPU:1, one launch (start us, length us, event | category | flops | bytes accessed | tf_op | source)
XLA Modules:
  0.0 94.6 jit_solution(6623101618002355910)
XLA Ops:
  0.7 1.1 %pad_maximum_fusion.5 = (f32[4,64,128]{2,1,0:T(8,128)S(1)}, f32[4,64,128]{2,1,0:T(8,128)S(1)}) fusion(f32[1,256,128]{2,1,0:T(8,128)} %bitcast.110, f32[3,256,128]{2,1,0:T(8,128)} %param.16), kind=kLoop, calls=%fused_computation.73 | loop fusion | flops 65536 | bytes 786432 | tf_op jit(solution)/shard_map/slice | solution.py:22
  1.8 4.5 %collective-permute-start = (f32[4,64,128]{2,1,0:T(8,128)S(1)}, f32[4,64,128]{2,1,0:T(8,128)S(1)}, u32[]{:S(2)}, u32[]{:S(2)}) collective-permute-start(f32[4,64,128]{2,1,0:T(8,128)S(1)} %get-tuple-element.206), channel_id=1, source_target_pairs={{0,1},{1,2},{2,3},{3,4},{4,5},{5,6},{6,7},{7,8},{8,9},{9,10},{10,1... | collective-permute-start | bytes 393224 | tf_op jit(solution)/shard_map/ppermute | solution.py:21
  6.3 1.9 %collective-permute-start.1 = (f32[4,64,128]{2,1,0:T(8,128)S(1)}, f32[4,64,128]{2,1,0:T(8,128)S(1)}, u32[]{:S(2)}, u32[]{:S(2)}) collective-permute-start(f32[4,64,128]{2,1,0:T(8,128)S(1)} %get-tuple-element.207), channel_id=1, source_target_pairs={{1,0},{2,1},{3,2},{4,3},{5,4},{6,5},{7,6},{8,7},{9,8},{10,9},{11,1... | collective-permute-start | bytes 393224 | tf_op jit(solution)/shard_map/ppermute | solution.py:24
  8.2 1.0 %constant_dynamic-update-slice_fusion.1 = f32[7,256,128]{2,1,0:T(8,128)S(1)} fusion(f32[3,256,128]{2,1,0:T(8,128)} %param.16), kind=kLoop, calls=%fused_computation.84 | loop fusion | bytes 786432
  9.3 0.1 reshape.273
  9.4 0.6 gather_fusion.1
  10.7 0.1 broadcast_select_fusion
  10.8 0.6 gather_fusion.2
  11.4 0.0 copy-start.9
  11.4 8.7 %copy.59 = f32[3,256,128]{0,2,1:T(8,128)} copy(f32[3,256,128]{2,1,0:T(8,128)S(1)} %copy-done) | data formatting | bytes 786432 | tf_op args[0]
  20.1 6.4 %gather_fusion.9 = f32[128,3]{1,0:T(8,128)S(1)} fusion(f32[3,32768]{0,1:T(8,128)} %bitcast.108, s32[1024]{0:T(1024)S(1)} %pad_clamp_fusion), kind=kCustom, calls=%fused_computation.12 | custom fusion | bytes 3584 | tf_op jit(solution)/shard_map/gather | solution.py:171
  26.5 0.1 copy.60
  26.6 1.2 %gather_fusion.10 = f32[128]{0:T(128)S(1)} fusion(f32[32768]{0:T(1024)S(1)} %bitcast.111, s32[1024]{0:T(1024)S(1)} %pad_clamp_fusion), kind=kCustom, calls=%fused_computation.13 | custom fusion | bytes 1536 | tf_op jit(solution)/shard_map/gather | solution.py:172
  27.8 1.1 %gather_fusion.11 = f32[128]{0:T(128)S(1)} fusion(f32[32768]{0:T(1024)S(1)} %bitcast.114, s32[1024]{0:T(1024)S(1)} %pad_clamp_fusion), kind=kCustom, calls=%fused_computation.14 | custom fusion | bytes 1536 | tf_op jit(solution)/shard_map/gather | solution.py:173
  28.9 1.1 %gather_fusion.12 = f32[128]{0:T(128)S(1)} fusion(f32[32768]{0:T(1024)S(1)} %bitcast.115, s32[1024]{0:T(1024)S(1)} %pad_clamp_fusion), kind=kCustom, calls=%fused_computation.15 | custom fusion | bytes 1536 | tf_op jit(solution)/shard_map/gather | solution.py:174
  30.1 0.2 convert_reduce_fusion
  30.3 0.4 copy.50
  30.8 0.7 gather_fusion.14
  31.5 0.6 gather_fusion
  32.2 0.1 fusion.17
  32.3 9.0 %while.20 = (s32[]{:T(128)}, f32[4,128]{1,0:T(4,128)S(1)}, f32[4,27,128]{2,1,0:T(8,128)S(1)}, f32[4,3,128]{2,1,0:T(4,128)S(1)}, f32[4,3,27,128]{3,2,0,1:T(8,128)...) while((s32[]{:T(128)}, f32[4,128]{1,0:T(4,128)S(1)}, f32[4,27,128]{2,1,0:T(8,128)S(1)}, ...), condition=%wide.region_3.5_spmd, body=%wide.region_0.4_spmd.sunk | while | flops 10617218 | bytes 3714157 | solution.py:109
  32.3 0.7 multiply_reduce_fusion.2
  33.0 1.4 %fusion.40 = f32[128]{0:T(128)S(1)} fusion(f32[128,27,128]{2,0,1:T(8,128)S(1)} %multiply_reduce_fusion.2, f32[128]{0:T(128)S(1)} %fusion.39, f32[27,128]{1,0:T(8,128)S(1)} %dynamic-slice_bitcast_fusion.12), kind=kLoop, calls=%fused_computation.27.clone.1 | loop fusion | flops 7077760 | bytes 1784320 | tf_op jit(solution)/shard_map/while/body/eval_jaxpr/reduce_sum | solution.py:56
  34.6 0.7 multiply_reduce_fusion.2
  35.3 1.4 %fusion.40 = f32[128]{0:T(128)S(1)} fusion(f32[128,27,128]{2,0,1:T(8,128)S(1)} %multiply_reduce_fusion.2, f32[128]{0:T(128)S(1)} %fusion.39, f32[27,128]{1,0:T(8,128)S(1)} %dynamic-slice_bitcast_fusion.12), kind=kLoop, calls=%fused_computation.27.clone.1 | loop fusion | flops 7077760 | bytes 1784320 | tf_op jit(solution)/shard_map/while/body/eval_jaxpr/reduce_sum | solution.py:56
  36.8 0.7 multiply_reduce_fusion.2
  37.5 1.4 %fusion.40 = f32[128]{0:T(128)S(1)} fusion(f32[128,27,128]{2,0,1:T(8,128)S(1)} %multiply_reduce_fusion.2, f32[128]{0:T(128)S(1)} %fusion.39, f32[27,128]{1,0:T(8,128)S(1)} %dynamic-slice_bitcast_fusion.12), kind=kLoop, calls=%fused_computation.27.clone.1 | loop fusion | flops 7077760 | bytes 1784320 | tf_op jit(solution)/shard_map/while/body/eval_jaxpr/reduce_sum | solution.py:56
  39.1 0.7 multiply_reduce_fusion.2
  39.8 1.4 %fusion.40 = f32[128]{0:T(128)S(1)} fusion(f32[128,27,128]{2,0,1:T(8,128)S(1)} %multiply_reduce_fusion.2, f32[128]{0:T(128)S(1)} %fusion.39, f32[27,128]{1,0:T(8,128)S(1)} %dynamic-slice_bitcast_fusion.12), kind=kLoop, calls=%fused_computation.27.clone.1 | loop fusion | flops 7077760 | bytes 1784320 | tf_op jit(solution)/shard_map/while/body/eval_jaxpr/reduce_sum | solution.py:56
  41.3 0.7 scatter_custom_fusion
  42.0 0.0 copy-start.1
  42.2 3.6 %collective-permute-start.2 = (f32[7,64,128]{2,1,0:T(8,128)S(1)}, f32[7,64,128]{2,1,0:T(8,128)S(1)}, u32[]{:S(2)}, u32[]{:S(2)}) collective-permute-start(f32[7,64,128]{2,1,0:T(8,128)S(1)} %get-tuple-element.204), channel_id=1, source_target_pairs={{0,1},{1,2},{2,3},{3,4},{4,5},{5,6},{6,7},{7,8},{8,9},{9,10},{10,1... | collective-permute-start | bytes 688136 | tf_op jit(solution)/shard_map/ppermute | solution.py:21
  45.8 1.9 %collective-permute-start.3 = (f32[7,64,128]{2,1,0:T(8,128)S(1)}, f32[7,64,128]{2,1,0:T(8,128)S(1)}, u32[]{:S(2)}, u32[]{:S(2)}) collective-permute-start(f32[7,64,128]{2,1,0:T(8,128)S(1)} %get-tuple-element.205), channel_id=1, source_target_pairs={{1,0},{2,1},{3,2},{4,3},{5,4},{6,5},{7,6},{8,7},{9,8},{10,9},{11,1... | collective-permute-start | bytes 688136 | tf_op jit(solution)/shard_map/ppermute | solution.py:24
  47.8 1.1 %gather_fusion.13 = f32[128]{0:T(128)S(1)} fusion(f32[32768]{0:T(1024)S(1)} %bitcast.109, s32[1024]{0:T(1024)S(1)} %pad_clamp_fusion), kind=kCustom, calls=%fused_computation.16 | custom fusion | bytes 1536 | tf_op jit(solution)/shard_map/gather | solution.py:175
  48.9 0.1 copy.61
  49.1 1.5 %scatter_custom_fusion.1 = f32[7,256]{0,1:T(8,128)} fusion(s32[128]{0:T(128)S(1)} %fusion.28, f32[128,7]{1,0:T(8,128)S(1)} %copy.61, f32[]{:T(128)} %constant.137.clone.1), kind=kCustom, calls=%fused_computation.80 | custom fusion | bytes 7172 | tf_op jit(solution)/shard_map/scatter | solution.py:184
  50.5 14.0 %all-to-all-start = ((f32[7,128,2]{0,2,1:T(2,128)}), f32[7,128,2]{0,2,1:T(2,128)S(1)}, u32[]{:S(2)}, u32[]{:S(2)}) async-start(f32[7,128,2]{0,2,1:T(2,128)} %bitcast.44), calls=%async_computation | async-start | bytes 262144 | tf_op jit(solution)/shard_map/all_to_all | solution.py:185
  64.5 0.6 gather_fusion.5
  65.1 0.6 gather_fusion.4
  65.7 8.9 %all-to-all-done = f32[7,128,2]{0,2,1:T(2,128)S(1)} async-done(((f32[7,128,2]{0,2,1:T(2,128)}), f32[7,128,2]{0,2,1:T(2,128)S(1)}, u32[]{:S(2)}, u32[]{:S(2)}) %all-to-all-start) | async-done | bytes 7200 | tf_op jit(solution)/shard_map/all_to_all | solution.py:185
  74.5 0.7 copy.62
  75.2 0.1 pad_maximum_fusion
  75.4 0.4 copy.54
  75.8 0.7 gather_fusion.15
  76.5 0.1 fusion.16
  76.6 0.1 maximum_bitcast_fusion
  76.7 0.6 gather_fusion.6
  77.3 0.6 gather_fusion.7
  78.0 0.6 gather_fusion.8
  78.6 0.6 gather_fusion.3
  79.2 14.6 %while.21 = (s32[]{:T(128)}, f32[4,3,128]{2,0,1:T(4,128)S(1)}, f32[4,27,128]{2,1,0:T(8,128)S(1)}, f32[4,128]{1,0:T(4,128)S(1)}, f32[4,128]{1,0:T(4,128)S(1)}, /*...) while((s32[]{:T(128)}, f32[4,3,128]{2,0,1:T(4,128)S(1)}, ...), condition=%wide.region_8.10_spmd, body=%wide.region_5.9_spmd.sunk | while | flops 19931648 | bytes 7402641 | solution.py:149
  79.3 0.7 fusion.43
  80.0 2.1 %add_multiply_fusion.2 = f32[128,27,128]{2,0,1:T(8,128)S(1)} fusion(f32[128,27,128]{2,0,1:T(8,128)S(1)} %fusion.43, f32[27,128]{1,0:T(8,128)S(1)} %get-tuple-element.321, f32[27,128]{1,0:T(8,128)S(1)} %get-tuple-element.322, f32[128]{0:T(128)S(1)} %get-tuple-element.323, f32[128]{0:T(128)S(1)} %get-tuple-element.324, f32[27,128]{1,0:T(8,128)S(1)} %get-tuple-element.325), kind=kLoop, calls=%fused_computation.42.clone.1 | loop fusion | flops 12386304 | bytes 3581440 | tf_op jit(solution)/shard_map/while/body/eval_jaxpr/mul | solution.py:69
  82.2 0.7 fusion.44
  83.0 0.7 fusion.43
  83.7 2.1 %add_multiply_fusion.2 = f32[128,27,128]{2,0,1:T(8,128)S(1)} fusion(f32[128,27,128]{2,0,1:T(8,128)S(1)} %fusion.43, f32[27,128]{1,0:T(8,128)S(1)} %get-tuple-element.321, f32[27,128]{1,0:T(8,128)S(1)} %get-tuple-element.322, f32[128]{0:T(128)S(1)} %get-tuple-element.323, f32[128]{0:T(128)S(1)} %get-tuple-element.324, f32[27,128]{1,0:T(8,128)S(1)} %get-tuple-element.325), kind=kLoop, calls=%fused_computation.42.clone.1 | loop fusion | flops 12386304 | bytes 3581440 | tf_op jit(solution)/shard_map/while/body/eval_jaxpr/mul | solution.py:69
  85.8 0.7 fusion.44
  86.6 0.7 fusion.43
  87.3 2.1 %add_multiply_fusion.2 = f32[128,27,128]{2,0,1:T(8,128)S(1)} fusion(f32[128,27,128]{2,0,1:T(8,128)S(1)} %fusion.43, f32[27,128]{1,0:T(8,128)S(1)} %get-tuple-element.321, f32[27,128]{1,0:T(8,128)S(1)} %get-tuple-element.322, f32[128]{0:T(128)S(1)} %get-tuple-element.323, f32[128]{0:T(128)S(1)} %get-tuple-element.324, f32[27,128]{1,0:T(8,128)S(1)} %get-tuple-element.325), kind=kLoop, calls=%fused_computation.42.clone.1 | loop fusion | flops 12386304 | bytes 3581440 | tf_op jit(solution)/shard_map/while/body/eval_jaxpr/mul | solution.py:69
  89.5 0.7 fusion.44
  90.3 0.7 fusion.43
  91.0 2.1 %add_multiply_fusion.2 = f32[128,27,128]{2,0,1:T(8,128)S(1)} fusion(f32[128,27,128]{2,0,1:T(8,128)S(1)} %fusion.43, f32[27,128]{1,0:T(8,128)S(1)} %get-tuple-element.321, f32[27,128]{1,0:T(8,128)S(1)} %get-tuple-element.322, f32[128]{0:T(128)S(1)} %get-tuple-element.323, f32[128]{0:T(128)S(1)} %get-tuple-element.324, f32[27,128]{1,0:T(8,128)S(1)} %get-tuple-element.325), kind=kLoop, calls=%fused_computation.42.clone.1 | loop fusion | flops 12386304 | bytes 3581440 | tf_op jit(solution)/shard_map/while/body/eval_jaxpr/mul | solution.py:69
  93.1 0.7 fusion.44
  93.9 0.7 multiply_bitcast_fusion
  (102 shorter events, 1.2 us)
Async XLA Ops:
  0.6 8.8 %copy-start = (f32[3,256,128]{2,1,0:T(8,128)S(1)}, f32[3,256,128]{2,1,0:T(8,128)}, u32[]{:S(2)}) copy-start(f32[3,256,128]{2,1,0:T(8,128)} %param.16) | copy-start | bytes 1179652
  0.6 10.0 %copy-start.3 = (f32[256,128]{1,0:T(8,128)S(1)}, f32[256,128]{1,0:T(8,128)}, u32[]{:S(2)}) copy-start(f32[256,128]{1,0:T(8,128)} %param.17) | copy-start | bytes 393220
  0.7 10.1 %copy-start.4 = (f32[256,128]{1,0:T(8,128)S(1)}, f32[256,128]{1,0:T(8,128)}, u32[]{:S(2)}) copy-start(f32[256,128]{1,0:T(8,128)} %param.18) | copy-start | bytes 393220
  0.7 8.6 %copy-start.7 = (s32[4]{0:T(128)S(1)}, s32[4]{0:T(128)}, u32[]{:S(2)}) copy-start(s32[4]{0:T(128)} %param.21) | copy-start | bytes 52
  0.7 8.6 %copy-start.6 = (s32[4,27]{1,0:T(4,128)S(1)}, s32[4,27]{1,0:T(4,128)}, u32[]{:S(2)}) copy-start(s32[4,27]{1,0:T(4,128)} %param.23) | copy-start | bytes 1300
  0.7 10.0 %copy-start.8 = (s32[128]{0:T(128)S(1)}, s32[128]{0:T(128)}, u32[]{:S(2)}) copy-start(s32[128]{0:T(128)} %param.24) | copy-start | bytes 1540
  1.8 28.5 %collective-permute-start = (f32[4,64,128]{2,1,0:T(8,128)S(1)}, f32[4,64,128]{2,1,0:T(8,128)S(1)}, u32[]{:S(2)}, u32[]{:S(2)}) collective-permute-start(f32[4,64,128]{2,1,0:T(8,128)S(1)} %get-tuple-element.206), channel_id=1, source_target_pairs={{0,1},{1,2},{2,3},{3,4},{4,5},{5,6},{6,7},{7,8},{8,9},{9,10},{10,1... | collective-permute-start | bytes 393224 | tf_op jit(solution)/shard_map/ppermute | solution.py:21
  6.3 24.0 %collective-permute-start.1 = (f32[4,64,128]{2,1,0:T(8,128)S(1)}, f32[4,64,128]{2,1,0:T(8,128)S(1)}, u32[]{:S(2)}, u32[]{:S(2)}) collective-permute-start(f32[4,64,128]{2,1,0:T(8,128)S(1)} %get-tuple-element.207), channel_id=1, source_target_pairs={{1,0},{2,1},{3,2},{4,3},{5,4},{6,5},{7,6},{8,7},{9,8},{10,9},{11,1... | collective-permute-start | bytes 393224 | tf_op jit(solution)/shard_map/ppermute | solution.py:24
  11.4 17.5 %copy-start.5 = (f32[256,128]{1,0:T(8,128)S(1)}, f32[256,128]{1,0:T(8,128)}, u32[]{:S(2)}) copy-start(f32[256,128]{1,0:T(8,128)} %param.19) | copy-start | bytes 393220
  11.4 18.7 %copy-start.9 = (s32[128,1]{0,1:T(1,128)S(1)}, s32[128,1]{0,1:T(1,128)}, u32[]{:S(2)}) copy-start(s32[128,1]{0,1:T(1,128)} %param.25) | copy-start | bytes 1540
  32.3 9.0 %copy-start.2 = (f32[256,128]{1,0:T(8,128)S(1)}, f32[256,128]{1,0:T(8,128)}, u32[]{:S(2)}) copy-start(f32[256,128]{1,0:T(8,128)} %param.20) | copy-start | bytes 393220
  42.0 33.3 %copy-start.1 = (f32[256,128]{1,0:T(8,128)}, f32[256,128]{1,0:T(8,128)S(1)}, u32[]{:S(2)}) copy-start(f32[256,128]{1,0:T(8,128)S(1)} %scatter_custom_fusion) | copy-start | bytes 393220
  42.2 33.0 %collective-permute-start.2 = (f32[7,64,128]{2,1,0:T(8,128)S(1)}, f32[7,64,128]{2,1,0:T(8,128)S(1)}, u32[]{:S(2)}, u32[]{:S(2)}) collective-permute-start(f32[7,64,128]{2,1,0:T(8,128)S(1)} %get-tuple-element.204), channel_id=1, source_target_pairs={{0,1},{1,2},{2,3},{3,4},{4,5},{5,6},{6,7},{7,8},{8,9},{9,10},{10,1... | collective-permute-start | bytes 688136 | tf_op jit(solution)/shard_map/ppermute | solution.py:21
  45.8 29.4 %collective-permute-start.3 = (f32[7,64,128]{2,1,0:T(8,128)S(1)}, f32[7,64,128]{2,1,0:T(8,128)S(1)}, u32[]{:S(2)}, u32[]{:S(2)}) collective-permute-start(f32[7,64,128]{2,1,0:T(8,128)S(1)} %get-tuple-element.205), channel_id=1, source_target_pairs={{1,0},{2,1},{3,2},{4,3},{5,4},{6,5},{7,6},{8,7},{9,8},{10,9},{11,1... | collective-permute-start | bytes 688136 | tf_op jit(solution)/shard_map/ppermute | solution.py:24
  50.5 24.0 %all-to-all-start = ((f32[7,128,2]{0,2,1:T(2,128)}), f32[7,128,2]{0,2,1:T(2,128)S(1)}, u32[]{:S(2)}, u32[]{:S(2)}) async-start(f32[7,128,2]{0,2,1:T(2,128)} %bitcast.44), calls=%async_computation | async-start | bytes 262144 | tf_op jit(solution)/shard_map/all_to_all | solution.py:185
where the time goes:
time: 94.9 us; the launch traced here: 94.6 us
  local copies, waits for them, and re-layouts  31.6 us (33%)
  starting transfers between devices  26 us (27%)
  other arithmetic  25.9 us (27%)
  waiting for transfers between devices  8.88 us (9%)
  between operations  1.78 us (2%)
    all_to_all x1, starting transfers between devices, local(): lax.all_to_all(outgoing, ('gx', 'gy'), split_axis=1, concat_axis=1, tiled...  14 us
    unnamed x26, local copies, waits for them, and re-layouts  10.5 us
    all_to_all x1, waiting for transfers between devices, local(): lax.all_to_all(outgoing, ('gx', 'gy'), split_axis=1, concat_axis=1, tiled...  8.87 us
    mul x4, other arithmetic, force_cell(): factor = other_mass[None] * (own_term + other_term)  8.53 us
    ppermute x2, starting transfers between devices, padded(): lax.ppermute(lax.slice_in_dim(block, block.shape[dim] - width, None, axis...  8.14 us
    gather x2, local copies, waits for them, and re-layouts, local(): positions.reshape(3, flat_count)[:, mig_source]  6.47 us
    reduce_sum x4, other arithmetic, density_cell(): jnp.sum(other_mass[None] * weights, axis=(1, 2))  5.79 us
    reduce_sum x8, other arithmetic, pair_geometry(): distance = jnp.sqrt(jnp.sum(separation * separation, axis=0))  5.34 us
  transfers between devices with their start and end apart: 5, of which 1 were waited for; matrix products, arithmetic and copies ran while one was open for 27% of the time, Pallas kernels for 0%

commit v1 on v0

v1 whole, which is shorter than its diff:
```python
import functools
import math

import jax
import jax.numpy as jnp
from jax import lax
from jax.experimental import pallas as pl
from jax.experimental.pallas import tpu as pltpu
from jax.sharding import PartitionSpec as P

CELLS = 256
LANES = 128
RIM = 64
EXT = CELLS + 2 * RIM
NBR = 27
PAD = 32
SLOTS = 4
ROWS = 128
NORM = 8.0 / math.pi
TINY = 1e-12
UNROLL = 27

F32 = jnp.float32
BF16 = jnp.bfloat16
MESH = pl.DeviceIdType.MESH
NT = (((1,), (1,)), ((), ()))
NN = (((1,), (0,)), ((), ()))


def dot(a, b, dims=NN):
    return lax.dot_general(a, b, dims, preferred_element_type=F32)


def parts(value, count):
    out = []
    for _ in range(count - 1):
        head = value.astype(BF16).astype(F32)
        out.append(head)
        value = value - head
    out.append(value.astype(BF16).astype(F32))
    return out


def exact(select, value, dims=NN):
    return sum(dot(select, part.astype(BF16), dims) for part in parts(value, 3))


def iota(shape, dim):
    return lax.broadcasted_iota(jnp.int32, shape, dim)


def kernel(
    n_gx,
    n_gy,
    act,
    cnt,
    nbr,
    src,
    pos,
    mas,
    smo,
    ent,
    den,
    src_row,
    dst_row,
    nbr_mat,
    o_den,
    o_acc,
    o_arr,
    own,
    ext,
    tiles,
    bpart,
    mtile,
    ai,
    aj,
    idt,
    rho,
    outb,
    st1,
    st2,
    st3,
    load_sem,
    rim_send,
    rim_recv,
    id_send,
    id_recv,
    rho_send,
    rho_recv,
    a_send,
    a_recv,
    b_send,
    b_recv,
):
    gx, gy = lax.axis_index("gx"), lax.axis_index("gy")
    n_dev = n_gx * n_gy
    me = gx * n_gy + gy
    prev, nxt = (me + n_dev - 1) % n_dev, (me + 1) % n_dev
    near = [(prev // n_gy, prev % n_gy), (nxt // n_gy, nxt % n_gy)]

    barrier = pltpu.get_barrier_semaphore()
    for target in near:
        pl.semaphore_signal(barrier, inc=1, device_id=target, device_id_type=MESH)
    for k in range(1, n_gy):
        pl.semaphore_signal(
            barrier, inc=1, device_id=(gx, (gy + k) % n_gy), device_id_type=MESH
        )
    for k in range(1, n_gx):
        pl.semaphore_signal(
            barrier, inc=1, device_id=((gx + k) % n_gx, gy), device_id_type=MESH
        )

    fields = [pos.at[0], pos.at[1], pos.at[2], mas, smo, ent, den]
    loads = [
        pltpu.make_async_copy(f, own.at[pl.ds(v * CELLS, CELLS)], load_sem.at[0, v])
        for v, f in enumerate(fields)
    ]
    fills = [
        pltpu.make_async_copy(f, ext.at[pl.ds(v * EXT + RIM, CELLS)], load_sem.at[1, v])
        for v, f in enumerate(fields)
    ]
    for copy in loads + fills:
        copy.start()

    base = me * CELLS
    sub8 = iota((8, LANES), 0)
    ids = jnp.full((8, LANES), -1, jnp.int32)
    for s in range(SLOTS):
        ids = jnp.where((sub8 == s) & (s < cnt[0]), act[s], ids)
    idt[0] = ids.astype(F32)
    ext[pl.ds(7 * EXT, EXT), :] = jnp.zeros((EXT, LANES), F32)
    own[pl.ds(7 * CELLS, CELLS), :] = jnp.zeros((CELLS, LANES), F32)

    dest = dst_row[...]
    place = (dest % n_gy) * n_gx + dest // n_gy
    to_dest = (iota((LANES, ROWS), 0) == place).astype(F32)
    earlier = (iota((ROWS, ROWS), 0) < iota((ROWS, ROWS), 1)).astype(F32)
    before = dot(to_dest.astype(BF16), earlier.astype(BF16))
    rank = jnp.sum(to_dest * before, axis=0, keepdims=True)
    to_dest = to_dest.astype(BF16)
    src_cell = src_row[...] // LANES
    src_lane = src_row[...] % LANES
    pick_lane = (iota((LANES, ROWS), 0) == src_lane).astype(F32).astype(BF16)
    from_slot = ((src_cell + base).astype(F32) == idt[0]).astype(F32)
    is_new = jnp.sum(from_slot, axis=0, keepdims=True)

    for copy in loads:
        copy.wait()

    lane8 = iota((8, LANES), 1)

    def mig_row(r, state):
        where_from = src[r]
        tile = own[pl.ds(where_from // LANES, 8, stride=CELLS), :]
        value = jnp.sum(
            jnp.where(lane8 == where_from % LANES, tile, 0.0), axis=1, keepdims=True
        )
        return jnp.where(lane8 == r, value, state)

    state = lax.fori_loop(0, ROWS, mig_row, jnp.zeros((8, LANES), F32), unroll=8)

    pl.semaphore_wait(barrier, 2 + n_gy - 1 + n_gx - 1)

    sends = []
    for side, target in enumerate(near):
        first = 0 if side == 0 else CELLS - RIM
        land = RIM + CELLS if side == 0 else 0
        for v, f in enumerate(fields):
            sends.append(
                pltpu.make_async_remote_copy(
                    src_ref=f.at[pl.ds(first, RIM)],
                    dst_ref=ext.at[pl.ds(v * EXT + land, RIM)],
                    send_sem=rim_send.at[side, v],
                    recv_sem=rim_recv.at[side, v],
                    device_id=target,
                    device_id_type=MESH,
                )
            )
        sends.append(
            pltpu.make_async_remote_copy(
                src_ref=idt.at[0],
                dst_ref=idt.at[2 - side],
                send_sem=id_send.at[side],
                recv_sem=id_recv.at[side],
                device_id=target,
                device_id_type=MESH,
            )
        )
    for copy in sends:
        copy.start()
    for copy in fills + sends:
        copy.wait()

    for s in range(SLOTS):
        def fetch(k, _, s=s):
            cell = jnp.clip(nbr[s, k] - (base - RIM), 0, EXT - 1)
            row = pl.multiple_of((s * PAD + k) * 8, 8)
            tiles[pl.ds(row, 8), :] = ext[pl.ds(cell, 8, stride=EXT), :]
            return 0

        lax.fori_loop(0, NBR, fetch, 0, unroll=9)
        tiles[(s * PAD + NBR) * 8 : (s + 1) * PAD * 8, :] = jnp.ones(
            ((PAD - NBR) * 8, LANES), F32
        )

    entries = SLOTS * PAD

    def field(v):
        return tiles[pl.ds(v, entries, stride=8), :]

    k_of = iota((entries, LANES), 0) % PAD
    offset = [k_of // 9 - 1, (k_of // 3) % 3 - 1, k_of % 3 - 1]
    x = [field(v) - 0.5 + offset[v].astype(F32) for v in range(3)]
    mass = field(3)
    length = field(4)
    inv_len = 1.0 / length
    inv2 = inv_len * inv_len
    n2 = x[0] * x[0] + x[1] * x[1] + x[2] * x[2]

    def put_b(values):
        for c, value in enumerate(values):
            for p, part in enumerate(parts(value, 3)):
                bpart[pl.ds(p * 8 + c, entries, stride=24), :] = part

    def put_m(values):
        for c, value in enumerate(values):
            for p, part in enumerate(parts(value, 2)):
                mtile[pl.ds(p * 8 + c, entries, stride=16), :] = part

    one = jnp.ones((entries, LANES), F32)
    bpart[...] = jnp.zeros_like(bpart)
    mtile[...] = jnp.zeros_like(mtile)
    put_b([x[0], x[1], x[2], n2, one])
    put_m([mass * x[0], mass * x[1], mass * x[2], mass])

    def mid(value, s):
        return value[s * PAD + NBR // 2 : s * PAD + NBR // 2 + 1, :]

    own_x, own_inv, own_len = [], [], []
    zero3 = jnp.zeros((3, LANES), F32)
    for s in range(SLOTS):
        xs = [mid(x[v], s) for v in range(3)]
        hi2, ns = mid(inv2, s), mid(n2, s)
        own_x.append(jnp.concatenate(xs + [jnp.zeros((5, LANES), F32)], axis=0))
        own_inv.append(mid(inv_len, s))
        scaled = jnp.concatenate([-2.0 * hi2 * v for v in xs] + [hi2, hi2 * ns, zero3], axis=0)
        plain = jnp.concatenate(
            [-2.0 * v for v in xs] + [jnp.ones((1, LANES), F32), ns, zero3], axis=0
        )
        for ref, tile in ((ai, scaled), (aj, plain)):
            h, m, l = parts(tile, 3)
            big = jnp.concatenate([h, h, m, m, h, l, jnp.zeros((80, LANES), F32)], axis=0)
            ref[s] = jnp.transpose(big).astype(BF16)

    def pair_pass(a_ref, function, terms):
        def slot(s):
            a = a_ref[s][:, :48]
            total = jnp.zeros((16, LANES), F32)
            for k in range(NBR):
                e = s * PAD + k
                t = bpart[e * 24 : e * 24 + 24, :]
                h, m, l = t[0:8], t[8:16], t[16:24]
                b = jnp.concatenate([h, m, h, m, l, h], axis=0).astype(BF16)
                q2 = jnp.maximum(dot(a, b), TINY)
                value = function(q2)
                lhs = mtile[e * 16 : e * 16 + 16, :].astype(BF16)
                high = value.astype(BF16)
                total += dot(lhs, high, NT)
                if terms == 2:
                    total += dot(lhs, (value - high.astype(F32)).astype(BF16), NT)
            return total[0:8] + total[8:16]

        return [slot(s) for s in range(SLOTS)]

    def weight(q2):
        q = q2 * lax.rsqrt(q2)
        u = jnp.maximum(1.0 - q, 0.0)
        v = jnp.maximum(u - q, 0.0)
        return (u + u) * (u * u) - v * (v * v)

    def slope(q2):
        inv_q = lax.rsqrt(q2)
        q = q2 * inv_q
        u = 1.0 - q
        v = jnp.maximum(u - q, 0.0)
        return jnp.minimum(jnp.maximum(inv_q - 1.0, 0.0), 1.0) * (u + v)

    sums = pair_pass(ai, weight, 2)
    rho_rows = []
    for s in range(SLOTS):
        rho_rows.append(NORM * sums[s][3:4] * own_inv[s] * own_inv[s] * own_inv[s])
    rho8 = jnp.concatenate(rho_rows + [jnp.ones((4, LANES), F32)], axis=0)
    rho[0] = rho8

    moved = jnp.sum(from_slot * exact_rows(rho8, pick_lane), axis=0, keepdims=True)
    fresh = jnp.where(is_new > 0.5, moved, state[6:7])
    full = jnp.where(sub8 == 6, fresh, state)
    ranked = jnp.concatenate(
        [
            jnp.where(rank < 0.5, full, 0.0),
            jnp.where(rank < 0.5, 0.0, full),
            jnp.zeros((112, LANES), F32),
        ],
        axis=0,
    )
    outb[...] = exact(to_dest, ranked, NT)

    rho_copies = [
        pltpu.make_async_remote_copy(
            src_ref=rho.at[0],
            dst_ref=rho.at[2 - side],
            send_sem=rho_send.at[side],
            recv_sem=rho_recv.at[side],
            device_id=target,
            device_id_type=MESH,
        )
        for side, target in enumerate(near)
    ]
    for copy in rho_copies:
        copy.start()
    first_stage = []
    for k in range(1, n_gy):
        other = (gy + k) % n_gy
        first_stage.append(
            pltpu.make_async_remote_copy(
                src_ref=outb.at[pl.ds(pl.multiple_of(other * n_gx, n_gx), n_gx)],
                dst_ref=st1.at[pl.ds(pl.multiple_of(gy * n_gx, n_gx), n_gx)],
                send_sem=a_send.at[k],
                recv_sem=a_recv.at[k],
                device_id=(gx, other),
                device_id_type=MESH,
            )
        )
    for copy in first_stage:
        copy.start()
    mine = pl.ds(pl.multiple_of(gy * n_gx, n_gx), n_gx)
    st1[mine, :] = outb[mine, :]

    table = ext[6 * EXT + RIM : 6 * EXT + RIM + CELLS, :]
    row_id = iota((CELLS, LANES), 0)
    for s in range(SLOTS):
        hit = (row_id == act[s] - base) & (s < cnt[0])
        table = jnp.where(hit, rho8[s : s + 1], table)
    o_den[...] = table

    own_force = pair_pass(ai, slope, 2)

    for copy in first_stage:
        copy.wait()
    for a in range(n_gx):
        st2[a * n_gy : (a + 1) * n_gy, :] = st1[pl.ds(a, n_gy, stride=n_gx), :]
    second_stage = []
    for k in range(1, n_gx):
        other = (gx + k) % n_gx
        second_stage.append(
            pltpu.make_async_remote_copy(
                src_ref=st2.at[pl.ds(pl.multiple_of(other * n_gy, n_gy), n_gy)],
                dst_ref=st3.at[pl.ds(pl.multiple_of(gx * n_gy, n_gy), n_gy)],
                send_sem=b_send.at[k],
                recv_sem=b_recv.at[k],
                device_id=(other, gy),
                device_id_type=MESH,
            )
        )
    for copy in second_stage:
        copy.start()
    mine = pl.ds(pl.multiple_of(gx * n_gy, n_gy), n_gy)
    st3[mine, :] = st2[mine, :]

    for copy in rho_copies:
        copy.wait()

    candidates = jnp.concatenate([idt[0], idt[1], idt[2]], axis=0)
    wanted = jnp.full((1, LANES), -2, jnp.int32)
    lane1 = iota((1, LANES), 1)
    spread = jnp.concatenate(
        [nbr_mat[...], jnp.zeros((SLOTS, LANES - NBR), jnp.int32)], axis=1
    )
    for s in range(SLOTS):
        line = spread[s : s + 1]
        if s:
            line = pltpu.roll(line, s * PAD, 1)
        wanted = jnp.where((lane1 >= s * PAD) & (lane1 < s * PAD + NBR), line, wanted)
    match = (candidates == wanted.astype(F32)).astype(F32)
    match = jnp.transpose(jnp.concatenate([match, jnp.zeros((104, LANES), F32)], axis=0))
    news = jnp.concatenate([rho[0], rho[1], rho[2], jnp.zeros((104, LANES), F32)], axis=0)
    patch = exact(match.astype(BF16), news)
    hits = jnp.sum(match, axis=1, keepdims=True)
    dens = jnp.where(hits > 0.5, patch, field(6))
    inv4 = inv2 * inv2
    factor = mass * field(5) * jnp.exp(jnp.log(dens) * (-1.0 / 3.0)) * (inv4 * inv_len)
    put_b([x[0] * inv2, x[1] * inv2, x[2] * inv2, n2 * inv2, inv2])
    put_m([factor * x[0], factor * x[1], factor * x[2], factor])

    other_force = pair_pass(aj, slope, 2)

    live = cnt[0]
    for s in range(SLOTS):
        own_s = sums_of(own_force[s], own_x[s])
        other_s = sums_of(other_force[s], own_x[s])
        entropy_i = mid(field(5), s)
        rho_i = mid(dens, s)
        front = entropy_i * jnp.exp(jnp.log(rho_i) * (-1.0 / 3.0))
        front = front * (mid(inv4, s) * own_inv[s])
        result = (6.0 * NORM) * (front * own_s + other_s)
        result = jnp.where(s < live, result, 0.0)
        o_acc[:, s, :] = result[0:3]

    for copy in second_stage:
        copy.wait()
    turned = jnp.transpose(st3[...])
    halves = jnp.concatenate([turned[0:8], turned[8:16]], axis=1)
    width = 2 * n_dev
    source = iota((2 * LANES, width), 0)
    column = iota((2 * LANES, width), 1)
    spot = (source % LANES) * 2 + source // LANES
    o_arr[...] = sum(
        dot(part.astype(BF16), (spot == column).astype(F32).astype(BF16))
        for part in parts(halves, 3)
    )[0:7]


def exact_rows(value, select):
    return sum(dot(part.astype(BF16), select) for part in parts(value, 3))


def sums_of(total, own_x):
    return own_x * total[3:4] - total


def local(
    n_gx,
    n_gy,
    positions,
    masses,
    smoothing,
    entropy,
    density,
    active_cells,
    active_count,
    neighbours,
    mig_source,
    mig_dest,
):
    smem = pl.BlockSpec(memory_space=pltpu.SMEM)
    vmem = pl.BlockSpec(memory_space=pltpu.VMEM)
    hbm = pl.BlockSpec(memory_space=pl.ANY)
    n_dev = n_gx * n_gy
    entries = SLOTS * PAD
    dma = pltpu.SemaphoreType.DMA
    return pl.pallas_call(
        functools.partial(kernel, n_gx, n_gy),
        out_shape=(
            jax.ShapeDtypeStruct((CELLS, LANES), F32),
            jax.ShapeDtypeStruct((3, SLOTS, LANES), F32),
            jax.ShapeDtypeStruct((7, 2 * n_dev), F32),
        ),
        in_specs=[smem] * 4 + [hbm] * 5 + [vmem] * 3,
        out_specs=(vmem, vmem, vmem),
        scratch_shapes=[
            pltpu.VMEM((8 * CELLS, LANES), F32),
            pltpu.VMEM((8 * EXT, LANES), F32),
            pltpu.VMEM((entries * 8, LANES), F32),
            pltpu.VMEM((entries * 24, LANES), F32),
            pltpu.VMEM((entries * 16, LANES), F32),
            pltpu.VMEM((SLOTS, LANES, LANES), BF16),
            pltpu.VMEM((SLOTS, LANES, LANES), BF16),
            pltpu.VMEM((3, 8, LANES), F32),
            pltpu.VMEM((3, 8, LANES), F32),
            pltpu.VMEM((LANES, LANES), F32),
            pltpu.VMEM((LANES, LANES), F32),
            pltpu.VMEM((LANES, LANES), F32),
            pltpu.VMEM((LANES, LANES), F32),
            dma((2, 7)),
            dma((2, 7)),
            dma((2, 7)),
            dma((2,)),
            dma((2,)),
            dma((2,)),
            dma((2,)),
            dma((n_gy,)),
            dma((n_gy,)),
            dma((n_gx,)),
            dma((n_gx,)),
        ],
        compiler_params=pltpu.CompilerParams(collective_id=0, has_side_effects=True),
    )(
        active_cells,
        active_count,
        neighbours,
        mig_source,
        positions,
        masses,
        smoothing,
        entropy,
        density,
        mig_source.reshape(1, ROWS),
        mig_dest.reshape(1, ROWS),
        neighbours,
    )


def solution(mesh):
    both = ("gx", "gy")
    placed = (
        P(None, both, None),
        P(both, None),
        P(both, None),
        P(both, None),
        P(both, None),
        P(both),
        P(both),
        P(both, None),
        P(both),
        P(both, None),
    )
    return jax.shard_map(
        functools.partial(local, mesh.shape["gx"], mesh.shape["gy"]),
        mesh=mesh,
        in_specs=placed,
        out_specs=(P(both, None), P(None, both, None), P(None, both)),
        check_vma=False,
    )
```

time: 94.9 us -> 52 us (0.55)
  the two profiles are of different devices: /device:TPU:1 before, /device:TPU:0 now
where the time goes in v1:
time: 52 us; the launch traced here: 51.8 us
  Pallas kernels  47.6 us (92%)
  local copies, waits for them, and re-layouts  2.88 us (6%)
  between operations  1.3 us (2%)
    pallas_call x1, Pallas kernels, local(): pl.pallas_call(functools.partial(kernel, n_gx, n_gy), out_shape=(jax.Shap...  47.6 us
    unnamed x7, local copies, waits for them, and re-layouts  2.88 us

profile of v1, /device:TPU:0, one launch (start us, length us, event | category | flops | bytes accessed | tf_op | source)
XLA Modules:
  0.0 51.8 jit_solution(15884681445131595775)
XLA Ops:
  1.3 47.6 %shard_map.121 = (f32[256,128]{1,0:T(8,128)}, f32[3,4,128]{2,1,0:T(4,128)}, f32[7,256]{1,0:T(8,128)}) custom-call(s32[4]{0:T(128)} %act.1, s32[1]{0:T(128)S(6)} %copy.16.cnt, s32[4,27]{1,0:T(4,128)} %nbr_mat.1, s32[128]{0:T(128)} %src.1, f32[3,256,128]{2,1,0:T(8,128)} %pos.1, f32[256,128]{1,0:T(8,128)} %mas.1, f32[256,128]{1,0:T(8,128)} %smo.1, ...), custom_call_target="tpu_custom_call" | custom-call | tf_op jit(solution)/shard_map/pallas_call | solution.py:451
  48.9 0.0 copy-start.1
  48.9 1.6 %copy.17 = f32[256,128]{1,0:T(8,128)} copy(f32[256,128]{1,0:T(8,128)} %get-tuple-element.6) | data formatting | bytes 262144
  50.5 0.0 copy-done.1
  50.5 0.0 copy-start
  50.5 0.6 %copy.18 = f32[3,4,128]{2,1,0:T(4,128)} copy(f32[3,4,128]{2,1,0:T(4,128)S(1)} %copy-done.1) | data formatting | bytes 12288
  51.1 0.1 copy-done
  51.2 0.6 %copy.19 = f32[7,256]{1,0:T(8,128)} copy(f32[7,256]{1,0:T(8,128)S(1)} %copy-done) | data formatting | bytes 14336
Async XLA Ops:
  48.9 1.6 %copy-start.1 = (f32[3,4,128]{2,1,0:T(4,128)S(1)}, f32[3,4,128]{2,1,0:T(4,128)}, u32[]{:S(2)}) copy-start(f32[3,4,128]{2,1,0:T(4,128)} %get-tuple-element.7) | copy-start | bytes 18436
  50.5 0.7 %copy-start = (f32[7,256]{1,0:T(8,128)S(1)}, f32[7,256]{1,0:T(8,128)}, u32[]{:S(2)}) copy-start(f32[7,256]{1,0:T(8,128)} %get-tuple-element.8) | copy-start | bytes 21508

commit v2 on v1

--- a/solution.py
+++ b/solution.py
@@ -18,7 +18,7 @@
 ROWS = 128
 NORM = 8.0 / math.pi
 TINY = 1e-12
-UNROLL = 27
+CHUNK = 32
 
 F32 = jnp.float32
 BF16 = jnp.bfloat16
@@ -64,16 +64,21 @@
     src_row,
     dst_row,
     nbr_mat,
-    o_den,
+    o_rho,
     o_acc,
     o_arr,
     own,
     ext,
+    ext2,
     tiles,
+    tiles2,
     bpart,
     mtile,
-    ai,
-    aj,
+    ab,
+    sq,
+    hi_part,
+    lo_part,
+    acc,
     idt,
     rho,
     outb,
@@ -111,12 +116,18 @@
         )
 
     fields = [pos.at[0], pos.at[1], pos.at[2], mas, smo, ent, den]
+
+    def place_of(v, row, rows):
+        if v < 4:
+            return ext.at[pl.ds(v * EXT + row, rows)]
+        return ext2.at[pl.ds((v - 4) * EXT + row, rows)]
+
     loads = [
         pltpu.make_async_copy(f, own.at[pl.ds(v * CELLS, CELLS)], load_sem.at[0, v])
         for v, f in enumerate(fields)
     ]
     fills = [
-        pltpu.make_async_copy(f, ext.at[pl.ds(v * EXT + RIM, CELLS)], load_sem.at[1, v])
+        pltpu.make_async_copy(f, place_of(v, RIM, CELLS), load_sem.at[1, v])
         for v, f in enumerate(fields)
     ]
     for copy in loads + fills:
@@ -128,7 +139,7 @@
     for s in range(SLOTS):
         ids = jnp.where((sub8 == s) & (s < cnt[0]), act[s], ids)
     idt[0] = ids.astype(F32)
-    ext[pl.ds(7 * EXT, EXT), :] = jnp.zeros((EXT, LANES), F32)
+    ext2[pl.ds(3 * EXT, EXT), :] = jnp.zeros((EXT, LANES), F32)
     own[pl.ds(7 * CELLS, CELLS), :] = jnp.zeros((CELLS, LANES), F32)
 
     dest = dst_row[...]
@@ -158,25 +169,36 @@
         return jnp.where(lane8 == r, value, state)
 
     state = lax.fori_loop(0, ROWS, mig_row, jnp.zeros((8, LANES), F32), unroll=8)
+    own_len = []
+    for s in range(SLOTS):
+        row = jnp.clip(act[s] - base, 0, CELLS - 1)
+        own_len.append(own[pl.ds(row + 4 * CELLS, 1), :])
+    for s in range(SLOTS):
+        for t in (tiles, tiles2):
+            t[(s * PAD + NBR) * 4 : (s + 1) * PAD * 4, :] = jnp.ones(
+                ((PAD - NBR) * 4, LANES), F32
+            )
+    bpart[...] = jnp.zeros_like(bpart)
+    mtile[...] = jnp.zeros_like(mtile)
 
     pl.semaphore_wait(barrier, 2 + n_gy - 1 + n_gx - 1)
 
-    sends = []
-    for side, target in enumerate(near):
+    def rim(side, v):
         first = 0 if side == 0 else CELLS - RIM
         land = RIM + CELLS if side == 0 else 0
-        for v, f in enumerate(fields):
-            sends.append(
-                pltpu.make_async_remote_copy(
-                    src_ref=f.at[pl.ds(first, RIM)],
-                    dst_ref=ext.at[pl.ds(v * EXT + land, RIM)],
-                    send_sem=rim_send.at[side, v],
-                    recv_sem=rim_recv.at[side, v],
-                    device_id=target,
-                    device_id_type=MESH,
-                )
-            )
-        sends.append(
+        return pltpu.make_async_remote_copy(
+            src_ref=fields[v].at[pl.ds(first, RIM)],
+            dst_ref=place_of(v, land, RIM),
+            send_sem=rim_send.at[side, v],
+            recv_sem=rim_recv.at[side, v],
+            device_id=near[side],
+            device_id_type=MESH,
+        )
+
+    early = [rim(side, v) for v in range(4) for side in range(2)]
+    late = [rim(side, v) for v in range(4, 7) for side in range(2)]
+    for side, target in enumerate(near):
+        late.append(
             pltpu.make_async_remote_copy(
                 src_ref=idt.at[0],
                 dst_ref=idt.at[2 - side],
@@ -186,41 +208,37 @@
                 device_id_type=MESH,
             )
         )
-    for copy in sends:
+    for copy in early + late:
         copy.start()
-    for copy in fills + sends:
+    for copy in fills + early:
         copy.wait()
 
-    for s in range(SLOTS):
-        def fetch(k, _, s=s):
-            cell = jnp.clip(nbr[s, k] - (base - RIM), 0, EXT - 1)
-            row = pl.multiple_of((s * PAD + k) * 8, 8)
-            tiles[pl.ds(row, 8), :] = ext[pl.ds(cell, 8, stride=EXT), :]
-            return 0
-
-        lax.fori_loop(0, NBR, fetch, 0, unroll=9)
-        tiles[(s * PAD + NBR) * 8 : (s + 1) * PAD * 8, :] = jnp.ones(
-            ((PAD - NBR) * 8, LANES), F32
-        )
+    def gather(into, out_of):
+        for s in range(SLOTS):
+            def fetch(k, _, s=s):
+                cell = jnp.clip(nbr[s, k] - (base - RIM), 0, EXT - 1)
+                into[pl.ds((s * PAD + k) * 4, 4), :] = out_of[pl.ds(cell, 4, stride=EXT), :]
+                return 0
+
+            lax.fori_loop(0, NBR, fetch, 0, unroll=9)
 
     entries = SLOTS * PAD
-
-    def field(v):
-        return tiles[pl.ds(v, entries, stride=8), :]
-
+    gather(tiles, ext)
     k_of = iota((entries, LANES), 0) % PAD
     offset = [k_of // 9 - 1, (k_of // 3) % 3 - 1, k_of % 3 - 1]
+
+    def field(v):
+        ref = tiles if v < 4 else tiles2
+        return ref[pl.ds(v % 4, entries, stride=4), :]
+
     x = [field(v) - 0.5 + offset[v].astype(F32) for v in range(3)]
     mass = field(3)
-    length = field(4)
-    inv_len = 1.0 / length
-    inv2 = inv_len * inv_len
     n2 = x[0] * x[0] + x[1] * x[1] + x[2] * x[2]
 
-    def put_b(values):
+    def put_b(at, values):
         for c, value in enumerate(values):
             for p, part in enumerate(parts(value, 3)):
-                bpart[pl.ds(p * 8 + c, entries, stride=24), :] = part
+                bpart[pl.ds(at * entries * 24 + p * 8 + c, entries, stride=24), :] = part
 
     def put_m(values):
         for c, value in enumerate(values):
@@ -228,64 +246,87 @@
                 mtile[pl.ds(p * 8 + c, entries, stride=16), :] = part
 
     one = jnp.ones((entries, LANES), F32)
-    bpart[...] = jnp.zeros_like(bpart)
-    mtile[...] = jnp.zeros_like(mtile)
-    put_b([x[0], x[1], x[2], n2, one])
+    put_b(0, [x[0], x[1], x[2], n2, one])
     put_m([mass * x[0], mass * x[1], mass * x[2], mass])
 
     def mid(value, s):
         return value[s * PAD + NBR // 2 : s * PAD + NBR // 2 + 1, :]
 
-    own_x, own_inv, own_len = [], [], []
+    own_x, own_inv = [], []
     zero3 = jnp.zeros((3, LANES), F32)
     for s in range(SLOTS):
         xs = [mid(x[v], s) for v in range(3)]
-        hi2, ns = mid(inv2, s), mid(n2, s)
+        inv = 1.0 / own_len[s]
+        hi2, ns = inv * inv, mid(n2, s)
         own_x.append(jnp.concatenate(xs + [jnp.zeros((5, LANES), F32)], axis=0))
-        own_inv.append(mid(inv_len, s))
+        own_inv.append(inv)
         scaled = jnp.concatenate([-2.0 * hi2 * v for v in xs] + [hi2, hi2 * ns, zero3], axis=0)
         plain = jnp.concatenate(
             [-2.0 * v for v in xs] + [jnp.ones((1, LANES), F32), ns, zero3], axis=0
         )
-        for ref, tile in ((ai, scaled), (aj, plain)):
+        for at, tile in ((s, scaled), (SLOTS + s, plain)):
             h, m, l = parts(tile, 3)
             big = jnp.concatenate([h, h, m, m, h, l, jnp.zeros((80, LANES), F32)], axis=0)
-            ref[s] = jnp.transpose(big).astype(BF16)
-
-    def pair_pass(a_ref, function, terms):
-        def slot(s):
-            a = a_ref[s][:, :48]
+            ab[at] = jnp.transpose(big).astype(BF16)
+
+    def make(step, k):
+        a_at = jnp.where(step < SLOTS, step, step - SLOTS)
+        b_at = jnp.where(step < 2 * SLOTS, step % SLOTS, step - SLOTS) * PAD
+        t = bpart[pl.ds(pl.multiple_of((b_at + k) * 24, 8), 24), :]
+        h, m, l = t[0:8], t[8:16], t[16:24]
+        b = jnp.concatenate([h, m, h, m, l, h], axis=0).astype(BF16)
+        sq[k * LANES : (k + 1) * LANES, :] = dot(ab[a_at][:, :48], b)
+
+    def pair_pass(number, function, signs):
+        def slot(s, _):
+            after = jnp.minimum(number * SLOTS + s + 1, 3 * SLOTS - 1)
             total = jnp.zeros((16, LANES), F32)
+
+            def work(k):
+                for r in range(k * LANES, (k + 1) * LANES, CHUNK):
+                    rows = slice(r, r + CHUNK)
+                    hi_part[rows, :], lo_part[rows, :] = function(
+                        jnp.maximum(sq[rows, :], TINY)
+                    )
+
+            def reduce(k):
+                e = s * PAD + k
+                rows = slice(k * LANES, (k + 1) * LANES)
+                lhs = mtile[pl.ds(pl.multiple_of(e * 16, 16), 16), :]
+                lhs = jnp.concatenate([lhs * f for f in signs], axis=1).astype(BF16)
+                return dot(
+                    lhs, jnp.concatenate([hi_part[rows, :], lo_part[rows, :]], axis=1), NT
+                )
+
             for k in range(NBR):
-                e = s * PAD + k
-                t = bpart[e * 24 : e * 24 + 24, :]
-                h, m, l = t[0:8], t[8:16], t[16:24]
-                b = jnp.concatenate([h, m, h, m, l, h], axis=0).astype(BF16)
-                q2 = jnp.maximum(dot(a, b), TINY)
-                value = function(q2)
-                lhs = mtile[e * 16 : e * 16 + 16, :].astype(BF16)
-                high = value.astype(BF16)
-                total += dot(lhs, high, NT)
-                if terms == 2:
-                    total += dot(lhs, (value - high.astype(F32)).astype(BF16), NT)
-            return total[0:8] + total[8:16]
-
-        return [slot(s) for s in range(SLOTS)]
+                work(k)
+                if k:
+                    total = total + reduce(k - 1)
+                    make(after, k - 1)
+            total = total + reduce(NBR - 1)
+            make(after, NBR - 1)
+            acc[s] = total[0:8] + total[8:16]
+            return 0
+
+        lax.fori_loop(0, SLOTS, slot, 0)
+        return [acc[s] for s in range(SLOTS)]
 
     def weight(q2):
         q = q2 * lax.rsqrt(q2)
         u = jnp.maximum(1.0 - q, 0.0)
         v = jnp.maximum(u - q, 0.0)
-        return (u + u) * (u * u) - v * (v * v)
+        return (u * u * u).astype(BF16), (v * v * v).astype(BF16)
 
     def slope(q2):
         inv_q = lax.rsqrt(q2)
         q = q2 * inv_q
-        u = 1.0 - q
-        v = jnp.maximum(u - q, 0.0)
-        return jnp.minimum(jnp.maximum(inv_q - 1.0, 0.0), 1.0) * (u + v)
-
-    sums = pair_pass(ai, weight, 2)
+        g = jnp.clip(inv_q, 1.0, 2.0) + jnp.maximum(-3.0 * q, jnp.minimum(q - 2.0, -1.0))
+        high = g.astype(BF16)
+        return high, (g - high.astype(F32)).astype(BF16)
+
+    for k in range(NBR):
+        make(0, k)
+    sums = pair_pass(0, weight, (2.0, -1.0))
     rho_rows = []
     for s in range(SLOTS):
         rho_rows.append(NORM * sums[s][3:4] * own_inv[s] * own_inv[s] * own_inv[s])
@@ -316,8 +357,6 @@
         )
         for side, target in enumerate(near)
     ]
-    for copy in rho_copies:
-        copy.start()
     first_stage = []
     for k in range(1, n_gy):
         other = (gy + k) % n_gy
@@ -331,19 +370,20 @@
                 device_id_type=MESH,
             )
         )
-    for copy in first_stage:
+    for copy in rho_copies + first_stage:
         copy.start()
     mine = pl.ds(pl.multiple_of(gy * n_gx, n_gx), n_gx)
     st1[mine, :] = outb[mine, :]
-
-    table = ext[6 * EXT + RIM : 6 * EXT + RIM + CELLS, :]
-    row_id = iota((CELLS, LANES), 0)
-    for s in range(SLOTS):
-        hit = (row_id == act[s] - base) & (s < cnt[0])
-        table = jnp.where(hit, rho8[s : s + 1], table)
-    o_den[...] = table
-
-    own_force = pair_pass(ai, slope, 2)
+    o_rho[...] = rho8
+
+    for copy in late:
+        copy.wait()
+    gather(tiles2, ext2)
+    inv_len = 1.0 / field(4)
+    inv2 = inv_len * inv_len
+    put_b(1, [x[0] * inv2, x[1] * inv2, x[2] * inv2, n2 * inv2, inv2])
+
+    own_force = pair_pass(1, slope, (1.0, 1.0))
 
     for copy in first_stage:
         copy.wait()
@@ -387,37 +427,39 @@
     patch = exact(match.astype(BF16), news)
     hits = jnp.sum(match, axis=1, keepdims=True)
     dens = jnp.where(hits > 0.5, patch, field(6))
-    inv4 = inv2 * inv2
-    factor = mass * field(5) * jnp.exp(jnp.log(dens) * (-1.0 / 3.0)) * (inv4 * inv_len)
-    put_b([x[0] * inv2, x[1] * inv2, x[2] * inv2, n2 * inv2, inv2])
+    inv5 = inv2 * inv2 * inv_len
+    front = field(5) * jnp.exp(jnp.log(dens) * (-1.0 / 3.0)) * inv5
+    factor = mass * front
     put_m([factor * x[0], factor * x[1], factor * x[2], factor])
 
-    other_force = pair_pass(aj, slope, 2)
-
-    live = cnt[0]
-    for s in range(SLOTS):
-        own_s = sums_of(own_force[s], own_x[s])
-        other_s = sums_of(other_force[s], own_x[s])
-        entropy_i = mid(field(5), s)
-        rho_i = mid(dens, s)
-        front = entropy_i * jnp.exp(jnp.log(rho_i) * (-1.0 / 3.0))
-        front = front * (mid(inv4, s) * own_inv[s])
-        result = (6.0 * NORM) * (front * own_s + other_s)
-        result = jnp.where(s < live, result, 0.0)
-        o_acc[:, s, :] = result[0:3]
+    other_force = pair_pass(2, slope, (1.0, 1.0))
+
+    for s in range(SLOTS):
+        result = mid(front, s) * sums_of(own_force[s], own_x[s])
+        result = (6.0 * NORM) * (result + sums_of(other_force[s], own_x[s]))
+        o_acc[:, s, :] = jnp.where(s < cnt[0], result, 0.0)[0:3]
 
     for copy in second_stage:
         copy.wait()
-    turned = jnp.transpose(st3[...])
+    o_arr[...] = st3[...]
+
+
+def finish(n_dev, act, cnt, base, den, rho, acc, rows, o_den, o_acc, o_arr):
+    o_den[...] = den[...]
+    for s in range(SLOTS):
+        @pl.when(s < cnt[0])
+        def _(s=s):
+            o_den[pl.ds(act[s] - base[0], 1), :] = rho[s : s + 1, :]
+
+    o_acc[...] = acc[...]
+    turned = jnp.transpose(rows[...])
     halves = jnp.concatenate([turned[0:8], turned[8:16]], axis=1)
     width = 2 * n_dev
     source = iota((2 * LANES, width), 0)
     column = iota((2 * LANES, width), 1)
     spot = (source % LANES) * 2 + source // LANES
-    o_arr[...] = sum(
-        dot(part.astype(BF16), (spot == column).astype(F32).astype(BF16))
-        for part in parts(halves, 3)
-    )[0:7]
+    spread = (spot == column).astype(F32).astype(BF16)
+    o_arr[...] = exact_rows(halves, spread)[0:7]
 
 
 def exact_rows(value, select):
@@ -448,23 +490,28 @@
     n_dev = n_gx * n_gy
     entries = SLOTS * PAD
     dma = pltpu.SemaphoreType.DMA
-    return pl.pallas_call(
+    rho, acc, rows = pl.pallas_call(
         functools.partial(kernel, n_gx, n_gy),
         out_shape=(
-            jax.ShapeDtypeStruct((CELLS, LANES), F32),
+            jax.ShapeDtypeStruct((8, LANES), F32),
             jax.ShapeDtypeStruct((3, SLOTS, LANES), F32),
-            jax.ShapeDtypeStruct((7, 2 * n_dev), F32),
+            jax.ShapeDtypeStruct((LANES, LANES), F32),
         ),
         in_specs=[smem] * 4 + [hbm] * 5 + [vmem] * 3,
         out_specs=(vmem, vmem, vmem),
         scratch_shapes=[
             pltpu.VMEM((8 * CELLS, LANES), F32),
-            pltpu.VMEM((8 * EXT, LANES), F32),
-            pltpu.VMEM((entries * 8, LANES), F32),
-            pltpu.VMEM((entries * 24, LANES), F32),
+            pltpu.VMEM((4 * EXT, LANES), F32),
+            pltpu.VMEM((4 * EXT, LANES), F32),
+            pltpu.VMEM((entries * 4, LANES), F32),
+            pltpu.VMEM((entries * 4, LANES), F32),
+            pltpu.VMEM((2 * entries * 24, LANES), F32),
             pltpu.VMEM((entries * 16, LANES), F32),
-            pltpu.VMEM((SLOTS, LANES, LANES), BF16),
-            pltpu.VMEM((SLOTS, LANES, LANES), BF16),
+            pltpu.VMEM((2 * SLOTS, LANES, LANES), BF16),
+            pltpu.VMEM((NBR * LANES, LANES), F32),
+            pltpu.VMEM((NBR * LANES, LANES), BF16),
+            pltpu.VMEM((NBR * LANES, LANES), BF16),
+            pltpu.VMEM((SLOTS, 8, LANES), F32),
             pltpu.VMEM((3, 8, LANES), F32),
             pltpu.VMEM((3, 8, LANES), F32),
             pltpu.VMEM((LANES, LANES), F32),
@@ -498,6 +545,17 @@
         mig_dest.reshape(1, ROWS),
         neighbours,
     )
+    base = (lax.axis_index(("gx", "gy")) * CELLS).astype(jnp.int32).reshape(1)
+    return pl.pallas_call(
+        functools.partial(finish, n_dev),
+        out_shape=(
+            jax.ShapeDtypeStruct((CELLS, LANES), F32),
+            jax.ShapeDtypeStruct((3, SLOTS, LANES), F32),
+            jax.ShapeDtypeStruct((7, 2 * n_dev), F32),
+        ),
+        in_specs=[smem] * 3 + [vmem] * 4,
+        out_specs=(vmem, vmem, vmem),
+    )(active_cells, active_count, base, density, rho, acc, rows)
 
 
 def solution(mesh):

time: 52 us -> 36.8 us (0.71)
  Pallas kernels: 47.6 us -> 35.3 us
  local copies, waits for them, and re-layouts: 2.88 us -> 0 us
    pallas_call x1, Pallas kernels: 47.6 us -> 33.5 us  [local(): pl.pallas_call(functools.partial(kernel, n_gx, n_gy), out_shape=(jax.Shap...]
    unnamed x7 -> x0, local copies, waits for them, and re-layouts: 2.88 us -> none
    pallas_call x0 -> x1, Pallas kernels: none -> 1.8 us  [local(): pl.pallas_call(functools.partial(finish, n_dev), out_shape=(jax.ShapeDtyp...]
where the time goes in v2:
time: 36.8 us; the launch traced here: 36.6 us
  Pallas kernels  35.3 us (96%)
  between operations  1.29 us (4%)
    pallas_call x1, Pallas kernels, local(): pl.pallas_call(functools.partial(kernel, n_gx, n_gy), out_shape=(jax.Shap...  33.5 us
    pallas_call x1, Pallas kernels, local(): pl.pallas_call(functools.partial(finish, n_dev), out_shape=(jax.ShapeDtyp...  1.8 us

profile of v2, /device:TPU:0, one launch (start us, length us, event | category | flops | bytes accessed | tf_op | source)
XLA Modules:
  0.0 36.6 jit_solution(15062513344332124018)
XLA Ops:
  1.3 33.5 %shard_map.121 = (f32[8,128]{1,0:T(8,128)}, f32[3,4,128]{2,1,0:T(4,128)}, f32[128,128]{1,0:T(8,128)}) custom-call(s32[4]{0:T(128)} %act.3, s32[1]{0:T(128)S(6)} %copy.13.cnt, s32[4,27]{1,0:T(4,128)} %nbr_mat.1, s32[128]{0:T(128)} %src.1, f32[3,256,128]{2,1,0:T(8,128)} %pos.1, f32[256,128]{1,0:T(8,128)} %mas.1, f32[256,128]{1,0:T(8,128)} %smo.1, ...), custom_call_target="tpu_custom_call" | custom-call | tf_op jit(solution)/shard_map/pallas_call | solution.py:493
  34.8 1.8 %shard_map.122 = (f32[256,128]{1,0:T(8,128)}, f32[3,4,128]{2,1,0:T(4,128)}, f32[7,256]{1,0:T(8,128)}) custom-call(s32[4]{0:T(128)} %act.3, s32[1]{0:T(128)S(6)} %copy.13.cnt, s32[1]{0:T(128)} %bitcast.base, f32[256,128]{1,0:T(8,128)} %den.3, f32[8,128]{1,0:T(8,128)} %get-tuple-element.6.rho, f32[3,4,128]{2,1,0:T(4,128)} %get-tuple-element.7.acc, ...), custom_call_target="tpu_custom_call" | custom-call | tf_op jit(solution)/shard_map/pallas_call | solution.py:549

commit v3 on v2

--- a/solution.py
+++ b/solution.py
@@ -52,21 +52,27 @@
 def kernel(
     n_gx,
     n_gy,
-    act,
-    cnt,
-    nbr,
-    src,
+    act_h,
+    cnt_h,
+    nbr_h,
+    src_h,
     pos,
     mas,
     smo,
     ent,
     den,
+    src_row_h,
+    dst_row_h,
+    o_rho,
+    o_acc,
+    o_arr,
+    act,
+    cnt,
+    nbr,
+    src,
     src_row,
     dst_row,
     nbr_mat,
-    o_rho,
-    o_acc,
-    o_arr,
     own,
     ext,
     ext2,
@@ -85,6 +91,7 @@
     st1,
     st2,
     st3,
+    small_sem,
     load_sem,
     rim_send,
     rim_recv,
@@ -103,6 +110,29 @@
     prev, nxt = (me + n_dev - 1) % n_dev, (me + 1) % n_dev
     near = [(prev // n_gy, prev % n_gy), (nxt // n_gy, nxt % n_gy)]
 
+    has = [me > 0, me < n_dev - 1]
+
+    def start(side, copies):
+        @pl.when(has[side])
+        def _():
+            for copy in copies:
+                copy.start()
+
+    def wait(side, copies):
+        @pl.when(has[side])
+        def _():
+            for copy in copies:
+                copy.wait_send()
+
+        @pl.when(has[1 - side])
+        def _():
+            for copy in copies:
+                copy.wait_recv()
+
+    for at in (1, 2):
+        idt[at] = jnp.full((8, LANES), -1.0, F32)
+        rho[at] = jnp.ones((8, LANES), F32)
+
     barrier = pltpu.get_barrier_semaphore()
     for target in near:
         pl.semaphore_signal(barrier, inc=1, device_id=target, device_id_type=MESH)
@@ -130,8 +160,52 @@
         pltpu.make_async_copy(f, place_of(v, RIM, CELLS), load_sem.at[1, v])
         for v, f in enumerate(fields)
     ]
-    for copy in loads + fills:
+    small = [
+        pltpu.make_async_copy(a, b, small_sem.at[i])
+        for i, (a, b) in enumerate(
+            [
+                (act_h, act),
+                (cnt_h, cnt),
+                (dst_row_h, dst_row),
+                (src_row_h, src_row),
+                (src_h, src),
+                (nbr_h, nbr),
+                (nbr_h, nbr_mat),
+            ]
+        )
+    ]
+    for copy in small + loads + fills:
         copy.start()
+    pl.semaphore_wait(barrier, 2 + n_gy - 1 + n_gx - 1)
+    def rim(side, v):
+        first = 0 if side == 0 else CELLS - RIM
+        land = RIM + CELLS if side == 0 else 0
+        return pltpu.make_async_remote_copy(
+            src_ref=fields[v].at[pl.ds(first, RIM)],
+            dst_ref=place_of(v, land, RIM),
+            send_sem=rim_send.at[side, v],
+            recv_sem=rim_recv.at[side, v],
+            device_id=near[side],
+            device_id_type=MESH,
+        )
+
+    early = [[rim(side, v) for v in range(4)] for side in range(2)]
+    late = [[rim(side, v) for v in range(4, 7)] for side in range(2)]
+    for side, target in enumerate(near):
+        late[side].append(
+            pltpu.make_async_remote_copy(
+                src_ref=idt.at[0],
+                dst_ref=idt.at[2 - side],
+                send_sem=id_send.at[side],
+                recv_sem=id_recv.at[side],
+                device_id=target,
+                device_id_type=MESH,
+            )
+        )
+    for side in range(2):
+        start(side, early[side])
+    for copy in small:
+        copy.wait()
 
     base = me * CELLS
     sub8 = iota((8, LANES), 0)
@@ -181,37 +255,11 @@
     bpart[...] = jnp.zeros_like(bpart)
     mtile[...] = jnp.zeros_like(mtile)
 
-    pl.semaphore_wait(barrier, 2 + n_gy - 1 + n_gx - 1)
-
-    def rim(side, v):
-        first = 0 if side == 0 else CELLS - RIM
-        land = RIM + CELLS if side == 0 else 0
-        return pltpu.make_async_remote_copy(
-            src_ref=fields[v].at[pl.ds(first, RIM)],
-            dst_ref=place_of(v, land, RIM),
-            send_sem=rim_send.at[side, v],
-            recv_sem=rim_recv.at[side, v],
-            device_id=near[side],
-            device_id_type=MESH,
-        )
-
-    early = [rim(side, v) for v in range(4) for side in range(2)]
-    late = [rim(side, v) for v in range(4, 7) for side in range(2)]
-    for side, target in enumerate(near):
-        late.append(
-            pltpu.make_async_remote_copy(
-                src_ref=idt.at[0],
-                dst_ref=idt.at[2 - side],
-                send_sem=id_send.at[side],
-                recv_sem=id_recv.at[side],
-                device_id=target,
-                device_id_type=MESH,
-            )
-        )
-    for copy in early + late:
-        copy.start()
-    for copy in fills + early:
+    for copy in fills:
         copy.wait()
+    for side in range(2):
+        wait(side, early[side])
+        start(side, late[side])
 
     def gather(into, out_of):
         for s in range(SLOTS):
@@ -277,7 +325,7 @@
         b = jnp.concatenate([h, m, h, m, l, h], axis=0).astype(BF16)
         sq[k * LANES : (k + 1) * LANES, :] = dot(ab[a_at][:, :48], b)
 
-    def pair_pass(number, function, signs):
+    def pair_pass(number, function, signs, first=0, last=SLOTS):
         def slot(s, _):
             after = jnp.minimum(number * SLOTS + s + 1, 3 * SLOTS - 1)
             total = jnp.zeros((16, LANES), F32)
@@ -308,7 +356,7 @@
             acc[s] = total[0:8] + total[8:16]
             return 0
 
-        lax.fori_loop(0, SLOTS, slot, 0)
+        lax.fori_loop(first, last, slot, 0)
         return [acc[s] for s in range(SLOTS)]
 
     def weight(q2):
@@ -370,20 +418,22 @@
                 device_id_type=MESH,
             )
         )
-    for copy in rho_copies + first_stage:
+    for side in range(2):
+        start(side, rho_copies[side : side + 1])
+    for copy in first_stage:
         copy.start()
     mine = pl.ds(pl.multiple_of(gy * n_gx, n_gx), n_gx)
     st1[mine, :] = outb[mine, :]
     o_rho[...] = rho8
 
-    for copy in late:
-        copy.wait()
+    for side in range(2):
+        wait(side, late[side])
     gather(tiles2, ext2)
     inv_len = 1.0 / field(4)
     inv2 = inv_len * inv_len
     put_b(1, [x[0] * inv2, x[1] * inv2, x[2] * inv2, n2 * inv2, inv2])
 
-    own_force = pair_pass(1, slope, (1.0, 1.0))
+    pair_pass(1, slope, (1.0, 1.0), 0, SLOTS - 1)
 
     for copy in first_stage:
         copy.wait()
@@ -406,9 +456,10 @@
         copy.start()
     mine = pl.ds(pl.multiple_of(gx * n_gy, n_gy), n_gy)
     st3[mine, :] = st2[mine, :]
-
-    for copy in rho_copies:
-        copy.wait()
+    own_force = pair_pass(1, slope, (1.0, 1.0), SLOTS - 1, SLOTS)
+
+    for side in range(2):
+        wait(side, rho_copies[side : side + 1])
 
     candidates = jnp.concatenate([idt[0], idt[1], idt[2]], axis=0)
     wanted = jnp.full((1, LANES), -2, jnp.int32)
@@ -444,17 +495,18 @@
     o_arr[...] = st3[...]
 
 
-def finish(n_dev, act, cnt, base, den, rho, acc, rows, o_den, o_acc, o_arr):
+def finish(n_gx, n_gy, act, cnt, den, rho, acc, rows, o_den, o_acc, o_arr):
+    base = (lax.axis_index("gx") * n_gy + lax.axis_index("gy")) * CELLS
     o_den[...] = den[...]
     for s in range(SLOTS):
         @pl.when(s < cnt[0])
         def _(s=s):
-            o_den[pl.ds(act[s] - base[0], 1), :] = rho[s : s + 1, :]
+            o_den[pl.ds(jnp.clip(act[s] - base, 0, CELLS - 1), 1), :] = rho[s : s + 1, :]
 
     o_acc[...] = acc[...]
     turned = jnp.transpose(rows[...])
     halves = jnp.concatenate([turned[0:8], turned[8:16]], axis=1)
-    width = 2 * n_dev
+    width = 2 * n_gx * n_gy
     source = iota((2 * LANES, width), 0)
     column = iota((2 * LANES, width), 1)
     spot = (source % LANES) * 2 + source // LANES
@@ -497,9 +549,16 @@
             jax.ShapeDtypeStruct((3, SLOTS, LANES), F32),
             jax.ShapeDtypeStruct((LANES, LANES), F32),
         ),
-        in_specs=[smem] * 4 + [hbm] * 5 + [vmem] * 3,
+        in_specs=[hbm] * 11,
         out_specs=(vmem, vmem, vmem),
         scratch_shapes=[
+            pltpu.SMEM((SLOTS,), jnp.int32),
+            pltpu.SMEM((1,), jnp.int32),
+            pltpu.SMEM((SLOTS, NBR), jnp.int32),
+            pltpu.SMEM((ROWS,), jnp.int32),
+            pltpu.VMEM((1, ROWS), jnp.int32),
+            pltpu.VMEM((1, ROWS), jnp.int32),
+            pltpu.VMEM((SLOTS, NBR), jnp.int32),
             pltpu.VMEM((8 * CELLS, LANES), F32),
             pltpu.VMEM((4 * EXT, LANES), F32),
             pltpu.VMEM((4 * EXT, LANES), F32),
@@ -518,6 +577,7 @@
             pltpu.VMEM((LANES, LANES), F32),
             pltpu.VMEM((LANES, LANES), F32),
             pltpu.VMEM((LANES, LANES), F32),
+            dma((7,)),
             dma((2, 7)),
             dma((2, 7)),
             dma((2, 7)),
@@ -543,19 +603,17 @@
         density,
         mig_source.reshape(1, ROWS),
         mig_dest.reshape(1, ROWS),
-        neighbours,
     )
-    base = (lax.axis_index(("gx", "gy")) * CELLS).astype(jnp.int32).reshape(1)
     return pl.pallas_call(
-        functools.partial(finish, n_dev),
+        functools.partial(finish, n_gx, n_gy),
         out_shape=(
             jax.ShapeDtypeStruct((CELLS, LANES), F32),
             jax.ShapeDtypeStruct((3, SLOTS, LANES), F32),
             jax.ShapeDtypeStruct((7, 2 * n_dev), F32),
         ),
-        in_specs=[smem] * 3 + [vmem] * 4,
+        in_specs=[smem] * 2 + [vmem] * 4,
         out_specs=(vmem, vmem, vmem),
-    )(active_cells, active_count, base, density, rho, acc, rows)
+    )(active_cells, active_count, density, rho, acc, rows)
 
 
 def solution(mesh):

time: 36.8 us -> 33.3 us (0.905)
  the two profiles are of different devices: /device:TPU:0 before, /device:TPU:1 now
where the time goes in v3:
time: 33.3 us; the launch traced here: 33.2 us
  Pallas kernels  31.9 us (96%)
  between operations  1.29 us (4%)
    pallas_call x1, Pallas kernels, local(): pl.pallas_call(functools.partial(kernel, n_gx, n_gy), out_shape=(jax.Shap...  30.1 us
    pallas_call x1, Pallas kernels, local(): pl.pallas_call(functools.partial(finish, n_gx, n_gy), out_shape=(jax.Shap...  1.8 us

profile of v3, /device:TPU:1, one launch (start us, length us, event | category | flops | bytes accessed | tf_op | source)
XLA Modules:
  0.0 33.2 jit_solution(6700743848637465530)
XLA Ops:
  1.3 30.1 %shard_map.121 = (f32[8,128]{1,0:T(8,128)}, f32[3,4,128]{2,1,0:T(4,128)}, f32[128,128]{1,0:T(8,128)}) custom-call(s32[4]{0:T(128)} %act.1, s32[1]{0:T(128)S(6)} %copy.13.cnt_h.cnt, s32[4,27]{1,0:T(4,128)} %nbr_h.1, s32[128]{0:T(128)} %src_h.1, f32[3,256,128]{2,1,0:T(8,128)} %pos.1, f32[256,128]{1,0:T(8,128)} %mas.1, f32[256,128]{1,0:T(8,128)} %smo.1, ...), custom_call_target="tpu_custom_call" | custom-call | tf_op jit(solution)/shard_map/pallas_call | solution.py:545
  31.4 1.8 %shard_map.122 = (f32[256,128]{1,0:T(8,128)}, f32[3,4,128]{2,1,0:T(4,128)}, f32[7,256]{1,0:T(8,128)}) custom-call(s32[4]{0:T(128)} %act.1, s32[1]{0:T(128)S(6)} %copy.13.cnt_h.cnt, f32[256,128]{1,0:T(8,128)} %den.3, f32[8,128]{1,0:T(8,128)} %get-tuple-element.6.rho, f32[3,4,128]{2,1,0:T(4,128)} %get-tuple-element.7.acc, f32[128,128]{1,0:T(8,128)} %get-tuple-element.8.rows), custom_call_target="tpu_custom_call" | custom-call | tf_op jit(solution)/shard_map/pallas_call | solution.py:607

commit v4 on v3

--- a/solution.py
+++ b/solution.py
@@ -424,7 +424,8 @@
         copy.start()
     mine = pl.ds(pl.multiple_of(gy * n_gx, n_gx), n_gx)
     st1[mine, :] = outb[mine, :]
-    o_rho[...] = rho8
+    o_rho[0:8, :] = rho8
+    o_rho[8:16, :] = idt[0]
 
     for side in range(2):
         wait(side, late[side])
@@ -495,14 +496,13 @@
     o_arr[...] = st3[...]
 
 
-def finish(n_gx, n_gy, act, cnt, den, rho, acc, rows, o_den, o_acc, o_arr):
+def finish(n_gx, n_gy, den, news, acc, rows, o_den, o_acc, o_arr):
     base = (lax.axis_index("gx") * n_gy + lax.axis_index("gy")) * CELLS
-    o_den[...] = den[...]
-    for s in range(SLOTS):
-        @pl.when(s < cnt[0])
-        def _(s=s):
-            o_den[pl.ds(jnp.clip(act[s] - base, 0, CELLS - 1), 1), :] = rho[s : s + 1, :]
-
+    row_id = (iota((CELLS, LANES), 0) + base).astype(F32)
+    table = den[...]
+    for s in range(SLOTS):
+        table = jnp.where(row_id == news[8 + s : 9 + s, :], news[s : s + 1, :], table)
+    o_den[...] = table
     o_acc[...] = acc[...]
     turned = jnp.transpose(rows[...])
     halves = jnp.concatenate([turned[0:8], turned[8:16]], axis=1)
@@ -536,16 +536,16 @@
     mig_source,
     mig_dest,
 ):
-    smem = pl.BlockSpec(memory_space=pltpu.SMEM)
     vmem = pl.BlockSpec(memory_space=pltpu.VMEM)
     hbm = pl.BlockSpec(memory_space=pl.ANY)
     n_dev = n_gx * n_gy
     entries = SLOTS * PAD
     dma = pltpu.SemaphoreType.DMA
+    keep = functools.partial(pltpu.with_memory_space_constraint, memory_space=pltpu.HBM)
     rho, acc, rows = pl.pallas_call(
         functools.partial(kernel, n_gx, n_gy),
         out_shape=(
-            jax.ShapeDtypeStruct((8, LANES), F32),
+            jax.ShapeDtypeStruct((16, LANES), F32),
             jax.ShapeDtypeStruct((3, SLOTS, LANES), F32),
             jax.ShapeDtypeStruct((LANES, LANES), F32),
         ),
@@ -590,19 +590,21 @@
             dma((n_gx,)),
             dma((n_gx,)),
         ],
-        compiler_params=pltpu.CompilerParams(collective_id=0, has_side_effects=True),
+        compiler_params=pltpu.CompilerParams(
+            collective_id=0, has_side_effects=True, vmem_limit_bytes=16 << 20
+        ),
     )(
-        active_cells,
+        keep(active_cells),
         active_count,
-        neighbours,
-        mig_source,
-        positions,
-        masses,
-        smoothing,
-        entropy,
-        density,
-        mig_source.reshape(1, ROWS),
-        mig_dest.reshape(1, ROWS),
+        keep(neighbours),
+        keep(mig_source),
+        keep(positions),
+        keep(masses),
+        keep(smoothing),
+        keep(entropy),
+        keep(density),
+        keep(mig_source.reshape(1, ROWS)),
+        keep(mig_dest.reshape(1, ROWS)),
     )
     return pl.pallas_call(
         functools.partial(finish, n_gx, n_gy),
@@ -611,9 +613,10 @@
             jax.ShapeDtypeStruct((3, SLOTS, LANES), F32),
             jax.ShapeDtypeStruct((7, 2 * n_dev), F32),
         ),
-        in_specs=[smem] * 2 + [vmem] * 4,
+        in_specs=[vmem] * 4,
         out_specs=(vmem, vmem, vmem),
-    )(active_cells, active_count, density, rho, acc, rows)
+        compiler_params=pltpu.CompilerParams(vmem_limit_bytes=4 << 20),
+    )(density, rho, acc, rows)
 
 
 def solution(mesh):

time: 33.3 us -> 31.7 us (0.952)
  Pallas kernels: 31.9 us -> 30.3 us
    pallas_call x1, Pallas kernels: 1.8 us -> 0.84 us  [local(): pl.pallas_call(functools.partial(finish, n_gx, n_gy), out_shape=(jax.Shap...]
    pallas_call x1, Pallas kernels: 30.1 us -> 29.4 us  [local(): pl.pallas_call(functools.partial(kernel, n_gx, n_gy), out_shape=(jax.Shap...]
where the time goes in v4:
time: 31.7 us; the launch traced here: 31.6 us
  Pallas kernels  30.3 us (96%)
  between operations  1.3 us (4%)
    pallas_call x1, Pallas kernels, local(): pl.pallas_call(functools.partial(kernel, n_gx, n_gy), out_shape=(jax.Shap...  29.4 us
    pallas_call x1, Pallas kernels, local(): pl.pallas_call(functools.partial(finish, n_gx, n_gy), out_shape=(jax.Shap...  0.84 us

profile of v4, /device:TPU:1, one launch (start us, length us, event | category | flops | bytes accessed | tf_op | source)
XLA Modules:
  0.0 31.6 jit_solution(4692335089374537988)
XLA Ops:
  1.3 0.0 copy-start
  1.3 29.4 %shard_map.121 = (f32[16,128]{1,0:T(8,128)S(1)}, f32[3,4,128]{2,1,0:T(4,128)S(1)}, f32[128,128]{1,0:T(8,128)S(1)}) custom-call(s32[4]{0:T(128)} %act_h.1, s32[1]{0:T(128)S(6)} %copy.13.cnt_h, s32[4,27]{1,0:T(4,128)} %nbr_h.1, s32[128]{0:T(128)} %src_h.1, f32[3,256,128]{2,1,0:T(8,128)} %pos.1, f32[256,128]{1,0:T(8,128)} %mas.1, f32[256,128]{1,0:T(8,128)} %smo.1, ...), custom_call_target="tpu_custom_call" | custom-call | tf_op jit(solution)/shard_map/pallas_call | solution.py:545
  30.7 0.0 copy-done
  30.8 0.8 %shard_map.122 = (f32[256,128]{1,0:T(8,128)}, f32[3,4,128]{2,1,0:T(4,128)}, f32[7,256]{1,0:T(8,128)}) custom-call(f32[256,128]{1,0:T(8,128)S(1)} %copy-done, f32[16,128]{1,0:T(8,128)S(1)} %get-tuple-element.6.news, f32[3,4,128]{2,1,0:T(4,128)S(1)} %get-tuple-element.7.acc, f32[128,128]{1,0:T(8,128)S(1)} %get-tuple-element.8.rows), custom_call_target="tpu_custom_call" | custom-call | tf_op jit(solution)/shard_map/pallas_call | solution.py:609
Async XLA Ops:
  1.3 29.5 %copy-start = (f32[256,128]{1,0:T(8,128)S(1)}, f32[256,128]{1,0:T(8,128)}, u32[]{:S(2)}) copy-start(f32[256,128]{1,0:T(8,128)} %den.3) | copy-start | bytes 393220

commit v5 on v4

--- a/solution.py
+++ b/solution.py
@@ -229,6 +229,17 @@
     from_slot = ((src_cell + base).astype(F32) == idt[0]).astype(F32)
     is_new = jnp.sum(from_slot, axis=0, keepdims=True)
 
+    wanted = jnp.full((1, LANES), -2, jnp.int32)
+    lane1 = iota((1, LANES), 1)
+    spread = jnp.concatenate(
+        [nbr_mat[...], jnp.zeros((SLOTS, LANES - NBR), jnp.int32)], axis=1
+    )
+    for s in range(SLOTS):
+        line = spread[s : s + 1]
+        if s:
+            line = pltpu.roll(line, s * PAD, 1)
+        wanted = jnp.where((lane1 >= s * PAD) & (lane1 < s * PAD + NBR), line, wanted)
+
     for copy in loads:
         copy.wait()
 
@@ -341,7 +352,7 @@
                 e = s * PAD + k
                 rows = slice(k * LANES, (k + 1) * LANES)
                 lhs = mtile[pl.ds(pl.multiple_of(e * 16, 16), 16), :]
-                lhs = jnp.concatenate([lhs * f for f in signs], axis=1).astype(BF16)
+                lhs = jnp.concatenate([lhs if f == 1.0 else lhs * f for f in signs], axis=1).astype(BF16)
                 return dot(
                     lhs, jnp.concatenate([hi_part[rows, :], lo_part[rows, :]], axis=1), NT
                 )
@@ -356,7 +367,7 @@
             acc[s] = total[0:8] + total[8:16]
             return 0
 
-        lax.fori_loop(first, last, slot, 0)
+        lax.fori_loop(first, last, slot, 0, unroll=True)
         return [acc[s] for s in range(SLOTS)]
 
     def weight(q2):
@@ -463,16 +474,6 @@
         wait(side, rho_copies[side : side + 1])
 
     candidates = jnp.concatenate([idt[0], idt[1], idt[2]], axis=0)
-    wanted = jnp.full((1, LANES), -2, jnp.int32)
-    lane1 = iota((1, LANES), 1)
-    spread = jnp.concatenate(
-        [nbr_mat[...], jnp.zeros((SLOTS, LANES - NBR), jnp.int32)], axis=1
-    )
-    for s in range(SLOTS):
-        line = spread[s : s + 1]
-        if s:
-            line = pltpu.roll(line, s * PAD, 1)
-        wanted = jnp.where((lane1 >= s * PAD) & (lane1 < s * PAD + NBR), line, wanted)
     match = (candidates == wanted.astype(F32)).astype(F32)
     match = jnp.transpose(jnp.concatenate([match, jnp.zeros((104, LANES), F32)], axis=0))
     news = jnp.concatenate([rho[0], rho[1], rho[2], jnp.zeros((104, LANES), F32)], axis=0)

time: 31.7 us -> 31.4 us (level)
  Pallas kernels: 30.3 us -> 29.9 us
    pallas_call x1, Pallas kernels: 29.4 us -> 29.1 us  [local(): pl.pallas_call(functools.partial(kernel, n_gx, n_gy), out_shape=(jax.Shap...]
where the time goes in v5:
time: 31.4 us; the launch traced here: 31.2 us
  Pallas kernels  29.9 us (95%)
  between operations  1.3 us (4%)
    pallas_call x1, Pallas kernels, local(): pl.pallas_call(functools.partial(kernel, n_gx, n_gy), out_shape=(jax.Shap...  29.1 us
    pallas_call x1, Pallas kernels, local(): pl.pallas_call(functools.partial(finish, n_gx, n_gy), out_shape=(jax.Shap...  0.84 us

profile of v5, /device:TPU:1, one launch (start us, length us, event | category | flops | bytes accessed | tf_op | source)
XLA Modules:
  0.0 31.2 jit_solution(13666363705535268867)
XLA Ops:
  1.3 0.0 copy-start
  1.3 29.1 %shard_map.121 = (f32[16,128]{1,0:T(8,128)S(1)}, f32[3,4,128]{2,1,0:T(4,128)S(1)}, f32[128,128]{1,0:T(8,128)S(1)}) custom-call(s32[4]{0:T(128)} %act_h.1, s32[1]{0:T(128)S(6)} %copy.13.cnt_h, s32[4,27]{1,0:T(4,128)} %nbr_h.1, s32[128]{0:T(128)} %src_h.1, f32[3,256,128]{2,1,0:T(8,128)} %pos.1, f32[256,128]{1,0:T(8,128)} %mas.1, f32[256,128]{1,0:T(8,128)} %smo.1, ...), custom_call_target="tpu_custom_call" | custom-call | tf_op jit(solution)/shard_map/pallas_call | solution.py:546
  30.4 0.0 copy-done
  30.4 0.8 %shard_map.122 = (f32[256,128]{1,0:T(8,128)}, f32[3,4,128]{2,1,0:T(4,128)}, f32[7,256]{1,0:T(8,128)}) custom-call(f32[256,128]{1,0:T(8,128)S(1)} %copy-done, f32[16,128]{1,0:T(8,128)S(1)} %get-tuple-element.6.news, f32[3,4,128]{2,1,0:T(4,128)S(1)} %get-tuple-element.7.acc, f32[128,128]{1,0:T(8,128)S(1)} %get-tuple-element.8.rows), custom_call_target="tpu_custom_call" | custom-call | tf_op jit(solution)/shard_map/pallas_call | solution.py:610
Async XLA Ops:
  1.3 29.1 %copy-start = (f32[256,128]{1,0:T(8,128)S(1)}, f32[256,128]{1,0:T(8,128)}, u32[]{:S(2)}) copy-start(f32[256,128]{1,0:T(8,128)} %den.3) | copy-start | bytes 393220

commit v6 on v5

--- a/solution.py
+++ b/solution.py
@@ -134,15 +134,15 @@
         rho[at] = jnp.ones((8, LANES), F32)
 
     barrier = pltpu.get_barrier_semaphore()
+    for k in range(1, n_gx):
+        pl.semaphore_signal(
+            barrier, inc=1, device_id=((gx + k) % n_gx, gy), device_id_type=MESH
+        )
     for target in near:
         pl.semaphore_signal(barrier, inc=1, device_id=target, device_id_type=MESH)
     for k in range(1, n_gy):
         pl.semaphore_signal(
             barrier, inc=1, device_id=(gx, (gy + k) % n_gy), device_id_type=MESH
-        )
-    for k in range(1, n_gx):
-        pl.semaphore_signal(
-            barrier, inc=1, device_id=((gx + k) % n_gx, gy), device_id_type=MESH
         )
 
     fields = [pos.at[0], pos.at[1], pos.at[2], mas, smo, ent, den]
@@ -391,6 +391,19 @@
         rho_rows.append(NORM * sums[s][3:4] * own_inv[s] * own_inv[s] * own_inv[s])
     rho8 = jnp.concatenate(rho_rows + [jnp.ones((4, LANES), F32)], axis=0)
     rho[0] = rho8
+    rho_copies = [
+        pltpu.make_async_remote_copy(
+            src_ref=rho.at[0],
+            dst_ref=rho.at[2 - side],
+            send_sem=rho_send.at[side],
+            recv_sem=rho_recv.at[side],
+            device_id=target,
+            device_id_type=MESH,
+        )
+        for side, target in enumerate(near)
+    ]
+    for side in range(2):
+        start(side, rho_copies[side : side + 1])
 
     moved = jnp.sum(from_slot * exact_rows(rho8, pick_lane), axis=0, keepdims=True)
     fresh = jnp.where(is_new > 0.5, moved, state[6:7])
@@ -405,17 +418,6 @@
     )
     outb[...] = exact(to_dest, ranked, NT)
 
-    rho_copies = [
-        pltpu.make_async_remote_copy(
-            src_ref=rho.at[0],
-            dst_ref=rho.at[2 - side],
-            send_sem=rho_send.at[side],
-            recv_sem=rho_recv.at[side],
-            device_id=target,
-            device_id_type=MESH,
-        )
-        for side, target in enumerate(near)
-    ]
     first_stage = []
     for k in range(1, n_gy):
         other = (gy + k) % n_gy
@@ -429,8 +431,6 @@
                 device_id_type=MESH,
             )
         )
-    for side in range(2):
-        start(side, rho_copies[side : side + 1])
     for copy in first_stage:
         copy.start()
     mine = pl.ds(pl.multiple_of(gy * n_gx, n_gx), n_gx)

time: 31.4 us -> 31.3 us (level)
  no operation moved by 1% of the time
where the time goes in v6:
time: 31.3 us; the launch traced here: 31.2 us
  Pallas kernels  29.9 us (96%)
  between operations  1.3 us (4%)
    pallas_call x1, Pallas kernels, local(): pl.pallas_call(functools.partial(kernel, n_gx, n_gy), out_shape=(jax.Shap...  29 us
    pallas_call x1, Pallas kernels, local(): pl.pallas_call(functools.partial(finish, n_gx, n_gy), out_shape=(jax.Shap...  0.84 us

profile of v6, /device:TPU:1, one launch (start us, length us, event | category | flops | bytes accessed | tf_op | source)
XLA Modules:
  0.0 31.2 jit_solution(1911987208904752015)
XLA Ops:
  1.3 0.0 copy-start
  1.3 29.0 %shard_map.121 = (f32[16,128]{1,0:T(8,128)S(1)}, f32[3,4,128]{2,1,0:T(4,128)S(1)}, f32[128,128]{1,0:T(8,128)S(1)}) custom-call(s32[4]{0:T(128)} %act_h.1, s32[1]{0:T(128)S(6)} %copy.13.cnt_h, s32[4,27]{1,0:T(4,128)} %nbr_h.1, s32[128]{0:T(128)} %src_h.1, f32[3,256,128]{2,1,0:T(8,128)} %pos.1, f32[256,128]{1,0:T(8,128)} %mas.1, f32[256,128]{1,0:T(8,128)} %smo.1, ...), custom_call_target="tpu_custom_call" | custom-call | tf_op jit(solution)/shard_map/pallas_call | solution.py:546
  30.3 0.0 copy-done
  30.3 0.8 %shard_map.122 = (f32[256,128]{1,0:T(8,128)}, f32[3,4,128]{2,1,0:T(4,128)}, f32[7,256]{1,0:T(8,128)}) custom-call(f32[256,128]{1,0:T(8,128)S(1)} %copy-done, f32[16,128]{1,0:T(8,128)S(1)} %get-tuple-element.6.news, f32[3,4,128]{2,1,0:T(4,128)S(1)} %get-tuple-element.7.acc, f32[128,128]{1,0:T(8,128)S(1)} %get-tuple-element.8.rows), custom_call_target="tpu_custom_call" | custom-call | tf_op jit(solution)/shard_map/pallas_call | solution.py:610
Async XLA Ops:
  1.3 29.0 %copy-start = (f32[256,128]{1,0:T(8,128)S(1)}, f32[256,128]{1,0:T(8,128)}, u32[]{:S(2)}) copy-start(f32[256,128]{1,0:T(8,128)} %den.3) | copy-start | bytes 393220
